TPU v7x, 32 devices: a whole 2x2x4 slice. The times are simulated.
32 devices in a mesh: gx: 2 (over x), gy: 4 (over y, core), gz: 4 (over z).
Axes of the slice: x: 2, y: 2, z: 4, core: 2. Of those that a mesh axis runs over, the one named last changes fastest.
Arguments:
- states: float32 [19, 32, 64, 512], P(None, 'gx', 'gy', 'gz'), may hold values from 0 to 1
- active: int32 [4, 4, 4], P('gx', 'gy', 'gz'), may hold values 0 or 1
- fibre_index: int32 [4, 4, 4], P('gx', 'gy', 'gz'), may hold values from 0 to 63
- fibre_angle: float32 [2, 64], replicated, may hold values from -3.140625 to 3.140625
- conduct: float32 [2, 64], replicated, may hold values from 0.05 to 0.3
- gate_half: float32 [17], replicated, may hold values from 0.1 to 0.9
- gate_slope: float32 [17], replicated, may hold values from 0.05 to 0.3
- gate_tau: float32 [17], replicated, may hold values from 2 to 60
- conductance: float32 [17], replicated, may hold values from 0.005 to 0.05
- reversal: float32 [17], replicated, may hold values from -1 to 1.5
- block_elem: int32 [16, 32, 16], P('gx', 'gy', 'gz'), may hold values from 0 to 8191, as said below
- block_weight: float32 [16, 32, 16], P('gx', 'gy', 'gz'), may hold values from 0.5 to 1.5
- node_disp: float32 [3, 16384], P(None, ('gx', 'gy', 'gz')), may hold values from -0.15 to 0.15
- elem_node: int32 [8, 8192], P(None, ('gx', 'gy', 'gz')), may hold values from 0 to 404, as said below
- elem_fibre: int32 [8192], P(('gx', 'gy', 'gz')), may hold values from 0 to 63
- material: float32 [3], replicated, may hold values from 0.5 to 2
Outputs:
- new_states: float32 [19, 32, 64, 512], P(None, 'gx', 'gy', 'gz')
- fine_disp: float32 [3, 32, 64, 512], P(None, 'gx', 'gy', 'gz')
- node_residual: float32 [3, 16384], P(None, ('gx', 'gy', 'gz'))
Inputs may be any that keep to these rules, and one draw needn't show every extreme that they name: `block_elem`: element numbers of the coarse partition: owner device e // 256, local element e % 256. Every element holds exactly one coupling block. Of the coupling blocks of one device at most 16 lie in elements of one owner device, and for every device some owner receives exactly 16 of them. `elem_node`: each column names eight distinct owner-local nodes of a hexahedral element of a structured partition, corner 4 i + 2 j + k at offset (i, j, k); neighbouring elements of one owner share nodes.
All inputs are finite; a program needn't handle non-finite values. No bound on the sum of `active` on one device may be relied on, other than what follows from the above.
Results may differ from a plain program's by a relative error of at most 0.0003.
Values sent between devices are 32-bit elements; how exact they have to be, the bound alone decides.
A program may use at most 64 MiB of HBM per device.

v0:
```python
import functools

import jax
import jax.numpy as jnp
from jax import lax
from jax.experimental import pallas as pl
from jax.experimental.pallas import tpu as pltpu
from jax.sharding import PartitionSpec as P

NSTATE = 19
TLX = 8
SBX = 2
SBY = 2
SBZ = 32
FINE_STEPS = 2
AXES = ("gx", "gy", "gz")
MESH = pl.DeviceIdType.MESH
LANES = 128
f32 = jnp.float32
bf16 = jnp.bfloat16
calcium_keep = 0.9
tension_half = 0.09
NN = (((1,), (0,)), ((), ()))
NT = (((1,), (1,)), ((), ()))


def mm(a, b, dims=NN):
    return lax.dot_general(a, b, dims, preferred_element_type=f32)


def parts3(x):
    x1 = x.astype(bf16)
    r1 = x - x1.astype(f32)
    x2 = r1.astype(bf16)
    x3 = (r1 - x2.astype(f32)).astype(bf16)
    return x1, x2, x3


def rows3(x):
    return jnp.concatenate([p.astype(f32) for p in parts3(x)], 0).astype(bf16)


def fold3(y):
    r = y.shape[0] // 3
    return y[:r] + y[r : 2 * r] + y[2 * r :]


def mm_right3(a, x, dims=NN):
    x1, x2, x3 = parts3(x)
    return mm(a, x1, dims) + mm(a, x2, dims) + mm(a, x3, dims)


def iota(shape, dim):
    return lax.broadcasted_iota(jnp.int32, shape, dim)


def column(row):
    pieces = [
        jnp.transpose(jnp.broadcast_to(row[:, i : i + LANES], (LANES, LANES)))
        for i in range(0, row.shape[1], LANES)
    ]
    return pieces[0] if len(pieces) == 1 else jnp.concatenate(pieces, 0)


def onehot(mask):
    return jnp.where(mask, 1.0, 0.0).astype(bf16)


def pick_rows(rows, shape):
    index = iota(shape, 0)
    out = jnp.zeros(shape, f32)
    for i, row in enumerate(rows):
        out = jnp.where(index == i, row, out)
    return out


def sigmoid(u):
    return 0.5 * jnp.tanh(0.5 * u) + 0.5


def frame_of(a, b):
    return jnp.cos(a) * jnp.cos(b), jnp.sin(a) * jnp.cos(b), jnp.sin(b)


def body(
    sizes,
    states,
    active,
    fibre_index,
    angle_s,
    angle_v,
    conduct,
    gate_half,
    gate_slope,
    gate_tau,
    conductance,
    reversal,
    ids_ref,
    weight_ref,
    node_disp,
    elem_node,
    elem_fibre,
    material,
    out,
    fine_out,
    resid_out,
    vs,
    flux,
    send_y,
    send_z,
    halo_x,
    halo_y,
    halo_z,
    corner_oh,
    corner_cd,
    slot_oh,
    pick_oh,
    owner_oh,
    rank_oh,
    ids_send,
    ids_got,
    val_send,
    val_got,
    ans_send,
    ans_got,
    face_send_sem,
    face_recv_sem,
    all_send_sem,
    all_recv_sem,
):
    mx, my, mz, seats, elem_count = sizes
    n = mx * my * mz
    nx, ny, nz = states.shape[1:]
    gates_n = NSTATE - 2
    bx, by, bz = nx // SBX, ny // SBY, nz // SBZ
    plane = bx * by
    blocks = plane * bz
    slots = n * seats
    tiles = nx // TLX
    node_count = node_disp.shape[1]
    corners = 8
    cx, cy, cz = (lax.axis_index(a) for a in AXES)
    me = (cx * my + cy) * mz + cz

    def coords(flat):
        return flat // (my * mz), (flat // mz) % my, flat % mz

    barrier = pltpu.get_barrier_semaphore()

    def greet(k, carry):
        pl.semaphore_signal(
            barrier, inc=1, device_id=coords((me + k) % n), device_id_type=MESH
        )
        return carry

    lax.fori_loop(1, n, greet, 0)

    def splat(value):
        return jnp.full((1, 1, LANES), value, f32)

    coef, live = [], []
    for t in range(tiles):
        index = fibre_index[0, 0, t]
        fx, fy, fz = frame_of(splat(angle_s[0, index]), splat(angle_s[1, index]))
        across = splat(conduct[1, index])
        spread = splat(conduct[0, index]) - across
        alive = splat(jnp.where(active[0, 0, t] > 0, 1.0, 0.0).astype(f32))
        live.append(alive)
        coef.append(
            [
                (across + spread * fx * fx) * alive,
                (across + spread * fy * fy) * alive,
                (across + spread * fz * fz) * alive,
                spread * fx * fy * alive,
                spread * fx * fz * alive,
                spread * fy * fz * alive,
            ]
        )

    chunk = 4

    def ionic(source, t):
        alive = live[t] > 0.5

        def step(i, carry):
            at = pl.ds(t * TLX + i * chunk, chunk)
            volt = source[0, at]
            current = jnp.zeros_like(volt)
            for g in range(gates_n):
                inv = 1.0 / splat(gate_slope[g])
                keep = jnp.exp(-1.0 / splat(gate_tau[g]))
                steady = sigmoid((volt - splat(gate_half[g])) * inv)
                old = source[1 + g, at]
                gate = steady + (old - steady) * keep
                current = current + splat(conductance[g]) * gate * (volt - splat(reversal[g]))
                out[1 + g, at] = jnp.where(alive, gate, old)
            old = source[NSTATE - 1, at]
            calcium = old * calcium_keep + (1.0 - calcium_keep) * sigmoid(8.0 * (volt - 0.5))
            out[NSTATE - 1, at] = jnp.where(alive, calcium, old)
            vs[at] = jnp.where(alive, volt - current, volt)
            return carry

        lax.fori_loop(0, TLX // chunk, step, 0)

    def face_copies(stage, low_x, high_x):
        near = [(cx, mx), (cy, my), (cz, mz)]
        made = []
        for dim in range(3):
            for side in range(2):
                if dim == 0:
                    src = high_x if side == 0 else low_x
                    dst = halo_x.at[stage, side]
                elif dim == 1:
                    src, dst = send_y.at[stage, side], halo_y.at[stage, side]
                else:
                    src, dst = send_z.at[stage, side], halo_z.at[stage, side]
                at, count = near[dim]
                to = [cx, cy, cz]
                to[dim] = (at + (1 if side == 0 else count - 1)) % count
                made.append(
                    pltpu.make_async_remote_copy(
                        src_ref=src,
                        dst_ref=dst,
                        send_sem=face_send_sem.at[stage, 2 * dim + side],
                        recv_sem=face_recv_sem.at[stage, 2 * dim + side],
                        device_id=tuple(to),
                        device_id_type=MESH,
                    )
                )
        return made

    def flat_z(a):
        return jnp.transpose(a.reshape(nx * ny, nz))

    def send_faces(stage, a_y, a_z, low_x, high_x):
        send_y[stage, 0] = a_y[:, ny - 1 : ny, :]
        send_y[stage, 1] = a_y[:, 0:1, :]
        turned = flat_z(a_z)
        send_z[stage, 0] = turned[nz - 1 : nz, :]
        send_z[stage, 1] = turned[0:1, :]
        copies = face_copies(stage, low_x, high_x)
        for c in copies:
            c.start()
        return copies

    def masked(value, inside):
        return jnp.where(inside, value, 0.0)

    def diff_x(a, stage):
        low = masked(halo_x[stage, 0], cx > 0)[None]
        high = masked(halo_x[stage, 1], cx < mx - 1)[None]
        up = jnp.concatenate([a[1:], high], 0)
        down = jnp.concatenate([low, a[:-1]], 0)
        return (up - down) * 0.5

    def diff_y(a, stage):
        low = masked(halo_y[stage, 0], cy > 0)
        high = masked(halo_y[stage, 1], cy < my - 1)
        row = iota((1, ny, nz), 1)
        down = jnp.where(row == 0, low, pltpu.roll(a, 1, 1))
        up = jnp.where(row == ny - 1, high, pltpu.roll(a, ny - 1, 1))
        return (up - down) * 0.5

    def diff_z(a, stage):
        low = masked(halo_z[stage, 0], cz > 0)
        high = masked(halo_z[stage, 1], cz < mz - 1)
        row = iota((nz, nx * ny), 0)
        edge = jnp.where(row == 0, low, jnp.where(row == nz - 1, high, 0.0))
        edge = jnp.transpose(edge).reshape(nx, ny, nz)
        lane = iota((1, 1, nz), 2)
        down = jnp.where(lane == 0, edge, pltpu.roll(a, 1, 2))
        up = jnp.where(lane == nz - 1, edge, pltpu.roll(a, nz - 1, 2))
        return (up - down) * 0.5

    def make_flux(stage):
        v = vs[...]
        gx, gy, gz = diff_x(v, stage), diff_y(v, stage), diff_z(v, stage)
        for t in range(tiles):
            at = slice(t * TLX, (t + 1) * TLX)
            xx, yy, zz, xy, xz, yz = coef[t]
            a, b, c = gx[at], gy[at], gz[at]
            flux[0, at] = xx * a + xy * b + xz * c
            flux[1, at] = xy * a + yy * b + yz * c
            flux[2, at] = xz * a + yz * b + zz * c

    def finish(stage):
        lap = diff_x(flux[0], stage) + diff_y(flux[1], stage) + diff_z(flux[2], stage)
        for t in range(tiles):
            at = slice(t * TLX, (t + 1) * TLX)
            out[0, at] = vs[at] + live[t] * lap[at]

    def all_copy(k, kind, src, dst):
        return pltpu.make_async_remote_copy(
            src_ref=src.at[(me + k) % n],
            dst_ref=dst.at[me],
            send_sem=all_send_sem.at[kind, k],
            recv_sem=all_recv_sem.at[kind, k],
            device_id=coords((me + k) % n),
            device_id_type=MESH,
        )

    def all_start(kind, src, dst):
        dst[pl.ds(me, 1)] = src[pl.ds(me, 1)]

        def go(k, carry):
            all_copy(k, kind, src, dst).start()
            return carry

        lax.fori_loop(1, n, go, 0)

    def all_wait(kind, src, dst):
        def go(k, carry):
            pltpu.make_async_remote_copy(
                src_ref=src.at[(me + k) % n],
                dst_ref=dst.at[(me + n - k) % n],
                send_sem=all_send_sem.at[kind, k],
                recv_sem=all_recv_sem.at[kind, k],
                device_id=coords((me + k) % n),
                device_id_type=MESH,
            ).wait()
            return carry

        lax.fori_loop(1, n, go, 0)

    per_row = LANES // seats
    groups = slots // LANES

    def lanes_of(got):
        pieces = []
        for g in range(groups):
            pieces.append(
                lax.fori_loop(
                    0,
                    per_row,
                    lambda r, acc, g=g: acc + got[g * per_row + r],
                    jnp.zeros((1, LANES), f32),
                )
            )
        return jnp.concatenate(pieces, 1)

    for t in range(tiles):
        ionic(states, t)
    shift = elem_count.bit_length() - 1

    def flat_row(ref):
        place = lax.rem(iota((by, blocks), 1), plane)
        spread = jnp.zeros((bz, blocks), f32)
        for i in range(bx):
            put = onehot(place == iota((by, blocks), 0) + i * by)
            for part in parts3(ref[i].astype(f32)):
                spread = spread + mm(part, put)
        mine = iota((bz, blocks), 1) // plane == iota((bz, blocks), 0)
        return jnp.sum(jnp.where(mine, spread, 0.0), axis=0, keepdims=True)

    ids = flat_row(ids_ref).astype(jnp.int32)
    weight_col = column(flat_row(weight_ref))
    owner = lax.shift_right_logical(ids, shift)
    local = ids - owner * elem_count
    owner_col = column(owner.astype(f32))
    owner_f = owner.astype(f32)
    owner_cols = jnp.concatenate([owner_col] * (blocks // LANES), 1)
    earlier = (owner_cols == owner_f) & (iota((blocks, blocks), 1) < iota((blocks, blocks), 0))
    rank = jnp.sum(jnp.where(earlier, 1.0, 0.0), axis=1, keepdims=True)
    offset = ((me % per_row) * seats).astype(f32)
    rank_hit = onehot(iota((blocks, LANES), 1).astype(f32) == rank + offset)
    rank_oh[...] = rank_hit
    owned = owner == iota((n, blocks), 0)
    owner_oh[...] = onehot(owned)
    slot_col = owner_col[:, 0:1] * seats + rank
    slot_oh[...] = onehot(iota((blocks, slots), 1).astype(f32) == slot_col)
    wanted = jnp.where(owned, local.astype(f32) + 1.0, 0.0).astype(bf16)
    ids_send[...] = mm(wanted, rank_hit).reshape(n, 1, LANES)

    pl.semaphore_wait(barrier, n - 1)
    v0 = vs[...]
    stage0 = send_faces(0, v0, v0, vs.at[0], vs.at[nx - 1])
    all_start(0, ids_send, ids_got)

    nodes = pick_rows([node_disp[i : i + 1, :] for i in range(3)], (8, node_count))
    nodes3 = rows3(nodes)
    for q in range(corners):
        hit = onehot(iota((node_count, elem_count), 0) == elem_node[q : q + 1, :])
        corner_oh[q] = hit
        corner_cd[q] = fold3(mm(nodes3, hit))

    for c in stage0:
        c.wait()
    make_flux(0)
    stage1 = send_faces(1, flux[1], flux[2], flux.at[0, 0], flux.at[0, nx - 1])

    all_wait(0, ids_send, ids_got)
    asked = column(lanes_of(ids_got)) - 1.0
    asked = jnp.concatenate([asked] * (elem_count // LANES), 1)
    pick_oh[...] = onehot(iota((slots, elem_count), 1).astype(f32) == asked)
    table = jnp.concatenate(
        [corner_cd[...].reshape(corners * 8, elem_count), jnp.zeros((LANES - corners * 8, elem_count), f32)],
        0,
    )
    ans_send[...] = mm_right3(pick_oh[...], table, NT).reshape(n, seats, LANES)
    all_start(1, ans_send, ans_got)

    for c in stage1:
        c.wait()
    finish(1)
    for t in range(tiles):
        ionic(out, t)
    v1 = vs[...]
    stage2 = send_faces(2, v1, v1, vs.at[0], vs.at[nx - 1])

    calcium = out[NSTATE - 1]
    square = calcium * calcium
    pull = (square / (square + tension_half)).reshape(bx, SBX, ny, nz)
    pull = (pull[:, 0] + pull[:, 1]).reshape(bx * ny, nz)
    pair = onehot(iota((plane, bx * ny), 1) // SBY == iota((plane, bx * ny), 0))
    pooled = mm_right3(pair, pull)
    strip = onehot(iota((nz, LANES), 0) // SBZ == iota((nz, LANES), 1))
    pooled = fold3(mm(rows3(pooled), strip)) * (1.0 / (SBX * SBY * SBZ))
    worth = jnp.concatenate(
        [
            jnp.broadcast_to(pooled[:, b : b + 1], (plane, LANES))
            for b in range(bz)
        ],
        0,
    )
    worth = jnp.where(rank_oh[...].astype(f32) > 0.5, worth * weight_col, 0.0)
    val_send[...] = mm_right3(owner_oh[...], worth).reshape(n, 1, LANES)
    all_start(2, val_send, val_got)

    angle = angle_v[...]
    fx, fy, fz = frame_of(angle[0:1, :], angle[1:2, :])
    entries = angle.shape[1]
    fibres = pick_rows([fx, fy, fz], (8, entries))
    which = onehot(iota((entries, elem_count), 0) == elem_fibre[...])
    frames = fold3(mm(rows3(fibres), which))
    frame = [frames[i : i + 1, :] for i in range(3)]
    grads = [
        [((2 * (q // 4) - 1) / 4), ((2 * (q // 2 % 2) - 1) / 4), ((2 * (q % 2) - 1) / 4)]
        for q in range(corners)
    ]
    sums = [sum(corner_cd[q] * grads[q][j] for q in range(corners)) for j in range(3)]
    d = [
        [sums[j][i : i + 1, :] + (1.0 if i == j else 0.0) for j in range(3)] for i in range(3)
    ]
    cof = [
        [
            d[(i + 1) % 3][(j + 1) % 3] * d[(i + 2) % 3][(j + 2) % 3]
            - d[(i + 1) % 3][(j + 2) % 3] * d[(i + 2) % 3][(j + 1) % 3]
            for j in range(3)
        ]
        for i in range(3)
    ]
    volume = d[0][0] * cof[0][0] + d[0][1] * cof[0][1] + d[0][2] * cof[0][2]
    inverse = 1.0 / volume
    logv = jnp.log(volume)
    shear, bulk, scale = material[0], material[1], material[2]
    passive = [
        [
            shear * (d[i][j] - cof[i][j] * inverse) + bulk * logv * (cof[i][j] * inverse)
            for j in range(3)
        ]
        for i in range(3)
    ]
    stretch = [
        scale * (d[i][0] * frame[0] + d[i][1] * frame[1] + d[i][2] * frame[2]) for i in range(3)
    ]

    for c in stage2:
        c.wait()
    make_flux(2)
    stage3 = send_faces(3, flux[1], flux[2], flux.at[0, 0], flux.at[0, nx - 1])

    all_wait(1, ans_send, ans_got)
    returned = ans_got[...].reshape(slots, LANES)
    near = mm_right3(slot_oh[...], returned)
    lane = iota((plane, nz), 1)
    strip_of = lane // SBZ
    xi = ((lane % SBZ).astype(f32) + 0.5) / SBZ
    for c in range(3):
        lines = []
        for ij in range(4):
            ends = []
            for k in range(2):
                col = (2 * ij + k) * 8 + c
                value = jnp.zeros((plane, nz), f32)
                for b in range(bz):
                    value = jnp.where(
                        strip_of == b, near[b * plane : (b + 1) * plane, col : col + 1], value
                    )
                ends.append(value)
            lines.append(ends[0] * (1.0 - xi) + ends[1] * xi)
        for iv in range(SBX):
            wx = (iv + 0.5) / SBX
            for jv in range(SBY):
                wy = (jv + 0.5) / SBY
                value = (
                    lines[0] * ((1 - wx) * (1 - wy))
                    + lines[1] * ((1 - wx) * wy)
                    + lines[2] * (wx * (1 - wy))
                    + lines[3] * (wx * wy)
                )
                for p in range(bx):
                    fine_out[c, SBX * p + iv, pl.ds(jv, by, stride=SBY), :] = value[
                        p * by : (p + 1) * by
                    ]

    for c in stage3:
        c.wait()
    finish(3)

    all_wait(2, val_send, val_got)
    arrived = jnp.broadcast_to(lanes_of(val_got), (8, slots))
    tension = fold3(mm(rows3(arrived), pick_oh[...]))[0:1, :]
    total = jnp.zeros((24, node_count), f32)
    stress = [
        [passive[i][j] + tension * stretch[i] * frame[j] for j in range(3)] for i in range(3)
    ]
    for q in range(corners):
        force = pick_rows(
            [
                stress[i][0] * grads[q][0] + stress[i][1] * grads[q][1] + stress[i][2] * grads[q][2]
                for i in range(3)
            ],
            (8, elem_count),
        )
        total = total + mm(rows3(force), corner_oh[q], NT)
    resid_out[...] = fold3(total)[0:3, :]


def shards(
    states,
    active,
    fibre_index,
    fibre_angle,
    conduct,
    gate_half,
    gate_slope,
    gate_tau,
    conductance,
    reversal,
    block_elem,
    block_weight,
    node_disp,
    elem_node,
    elem_fibre,
    material,
):
    mx, my, mz = (lax.axis_size(a) for a in AXES)
    n = mx * my * mz
    elem_count = elem_node.shape[1]
    node_count = node_disp.shape[1]
    nx, ny, nz = states.shape[1:]
    bx, by, bz = block_elem.shape
    blocks = bx * by * bz
    seats = max(2 * blocks // n, 8)
    slots = n * seats
    ids = block_elem.transpose(0, 2, 1)
    weight = block_weight.transpose(0, 2, 1)
    vmem = pl.BlockSpec(memory_space=pltpu.VMEM)
    smem = pl.BlockSpec(memory_space=pltpu.SMEM)
    stages = 2 * FINE_STEPS
    return pl.pallas_call(
        functools.partial(body, (mx, my, mz, seats, elem_count)),
        out_shape=(
            jax.ShapeDtypeStruct(states.shape, f32),
            jax.ShapeDtypeStruct((3, nx, ny, nz), f32),
            jax.ShapeDtypeStruct((3, node_count), f32),
        ),
        in_specs=[vmem, smem, smem, smem, vmem] + [smem] * 6 + [vmem] * 5 + [smem],
        out_specs=(vmem, vmem, vmem),
        scratch_shapes=[
            pltpu.VMEM((nx, ny, nz), f32),
            pltpu.VMEM((3, nx, ny, nz), f32),
            pltpu.VMEM((stages, 2, nx, 1, nz), f32),
            pltpu.VMEM((stages, 2, 1, nx * ny), f32),
            pltpu.VMEM((stages, 2, ny, nz), f32),
            pltpu.VMEM((stages, 2, nx, 1, nz), f32),
            pltpu.VMEM((stages, 2, 1, nx * ny), f32),
            pltpu.VMEM((8, node_count, elem_count), bf16),
            pltpu.VMEM((8, 8, elem_count), f32),
            pltpu.VMEM((blocks, slots), bf16),
            pltpu.VMEM((slots, elem_count), bf16),
            pltpu.VMEM((n, blocks), bf16),
            pltpu.VMEM((blocks, LANES), bf16),
            pltpu.VMEM((n, 1, LANES), f32),
            pltpu.VMEM((n, 1, LANES), f32),
            pltpu.VMEM((n, 1, LANES), f32),
            pltpu.VMEM((n, 1, LANES), f32),
            pltpu.VMEM((n, seats, LANES), f32),
            pltpu.VMEM((n, seats, LANES), f32),
            pltpu.SemaphoreType.DMA((stages, 6)),
            pltpu.SemaphoreType.DMA((stages, 6)),
            pltpu.SemaphoreType.DMA((3, n)),
            pltpu.SemaphoreType.DMA((3, n)),
        ],
        compiler_params=pltpu.CompilerParams(
            collective_id=0, has_side_effects=True, vmem_limit_bytes=60 * 1024 * 1024
        ),
        name="step",
    )(
        states,
        active.transpose(1, 2, 0),
        fibre_index.transpose(1, 2, 0),
        fibre_angle,
        fibre_angle,
        conduct,
        gate_half,
        gate_slope,
        gate_tau,
        conductance,
        reversal,
        ids,
        weight,
        node_disp,
        elem_node,
        elem_fibre.reshape(1, elem_count),
        material,
    )


def solution(mesh):
    in_specs = (
        P(None, "gx", "gy", "gz"),
        P("gx", "gy", "gz"),
        P("gx", "gy", "gz"),
        P(),
        P(),
        P(),
        P(),
        P(),
        P(),
        P(),
        P("gx", "gy", "gz"),
        P("gx", "gy", "gz"),
        P(None, ("gx", "gy", "gz")),
        P(None, ("gx", "gy", "gz")),
        P(("gx", "gy", "gz")),
        P(),
    )
    out_specs = (P(None, "gx", "gy", "gz"), P(None, "gx", "gy", "gz"), P(None, ("gx", "gy", "gz")))
    return jax.shard_map(shards, mesh=mesh, in_specs=in_specs, out_specs=out_specs, check_vma=False)
```

profile of v0, /device:TPU:0, one launch (start us, length us, event | category | flops | bytes accessed | tf_op | source)
XLA Modules:
  0.0 35.3 jit_solution(339581504646815656)
XLA Ops:
  0.6 29.9 %step.1 = (f32[19,16,16,128]{3,2,1,0:T(8,128)}, f32[3,16,16,128]{3,2,1,0:T(8,128)}, f32[3,512]{1,0:T(4,128)}) custom-call(f32[19,16,16,128]{3,2,1,0:T(8,128)} %states.1, s32[1,1,2]{2,1,0:T(1,128)} %bitcast.8, s32[1,1,2]{2,1,0:T(1,128)} %bitcast.9, f32[2,64]{1,0:T(2,128)} %angle_v.1, f32[2,64]{1,0:T(2,128)} %angle_v.1, f32[2,64]{1,0:T(2,128)} %conduct.1, ...), custom_call_target="tpu_custom_call" | custom-call | tf_op jit(solution)/shard_map/step/pallas_call | solution.py:561
  30.5 0.0 copy-start
  30.5 0.0 copy-start.1
  30.6 3.4 %copy.22 = f32[19,16,16,128]{3,2,1,0:T(8,128)} copy(f32[19,16,16,128]{3,2,1,0:T(8,128)} %get-tuple-element.6) | data formatting | bytes 4980736
  34.0 0.0 copy-done
  34.0 0.7 %copy.23 = f32[3,16,16,128]{3,2,1,0:T(8,128)} copy(f32[3,16,16,128]{3,2,1,0:T(8,128)S(1)} %copy-done) | data formatting | bytes 786432
  34.7 0.0 copy-done.1
  34.7 0.6 %copy.24 = f32[3,512]{1,0:T(4,128)} copy(f32[3,512]{1,0:T(4,128)S(1)} %copy-done.1) | data formatting | bytes 12288
Async XLA Ops:
  30.5 3.4 %copy-start = (f32[3,16,16,128]{3,2,1,0:T(8,128)S(1)}, f32[3,16,16,128]{3,2,1,0:T(8,128)}, u32[]{:S(2)}) copy-start(f32[3,16,16,128]{3,2,1,0:T(8,128)} %get-tuple-element.7) | copy-start | bytes 1179652
  30.5 4.2 %copy-start.1 = (f32[3,512]{1,0:T(4,128)S(1)}, f32[3,512]{1,0:T(4,128)}, u32[]{:S(2)}) copy-start(f32[3,512]{1,0:T(4,128)} %get-tuple-element.8) | copy-start | bytes 18436
where the time goes:
time: 35.5 us; the launch traced here: 35.3 us
  Pallas kernels  29.9 us (84%)
  local copies, waits for them, and re-layouts  4.77 us (13%)
  between operations  0.66 us (2%)
    pallas_call x1, Pallas kernels, shards(): pl.pallas_call(functools.partial(body, (mx, my, mz, seats, elem_count)),...  29.9 us
    unnamed x7, local copies, waits for them, and re-layouts  4.77 us

commit v1 on v0

--- a/solution.py
+++ b/solution.py
@@ -72,6 +72,10 @@
     for i, row in enumerate(rows):
         out = jnp.where(index == i, row, out)
     return out
+
+
+def lane_gather(x, index):
+    return jnp.take_along_axis(x, index, axis=1, mode="promise_in_bounds")
 
 
 def sigmoid(u):
@@ -376,12 +380,19 @@
     stage0 = send_faces(0, v0, v0, vs.at[0], vs.at[nx - 1])
     all_start(0, ids_send, ids_got)
 
-    nodes = pick_rows([node_disp[i : i + 1, :] for i in range(3)], (8, node_count))
-    nodes3 = rows3(nodes)
+    index = elem_node[...]
+    for h in range(0, elem_count, LANES):
+        ix = index[:, h : h + LANES]
+        low, high = ix % LANES, ix // LANES
+        for i in range(3):
+            value = jnp.zeros((corners, LANES), f32)
+            for g in range(node_count // LANES):
+                row = jnp.broadcast_to(node_disp[i : i + 1, g * LANES : (g + 1) * LANES], (corners, LANES))
+                value = jnp.where(high == g, lane_gather(row, low), value)
+            corner_cd[i, :, h : h + LANES] = value
     for q in range(corners):
         hit = onehot(iota((node_count, elem_count), 0) == elem_node[q : q + 1, :])
         corner_oh[q] = hit
-        corner_cd[q] = fold3(mm(nodes3, hit))
 
     for c in stage0:
         c.wait()
@@ -393,7 +404,7 @@
     asked = jnp.concatenate([asked] * (elem_count // LANES), 1)
     pick_oh[...] = onehot(iota((slots, elem_count), 1).astype(f32) == asked)
     table = jnp.concatenate(
-        [corner_cd[...].reshape(corners * 8, elem_count), jnp.zeros((LANES - corners * 8, elem_count), f32)],
+        [corner_cd[...].reshape(corners * 3, elem_count), jnp.zeros((LANES - corners * 3, elem_count), f32)],
         0,
     )
     ans_send[...] = mm_right3(pick_oh[...], table, NT).reshape(n, seats, LANES)
@@ -437,7 +448,7 @@
         [((2 * (q // 4) - 1) / 4), ((2 * (q // 2 % 2) - 1) / 4), ((2 * (q % 2) - 1) / 4)]
         for q in range(corners)
     ]
-    sums = [sum(corner_cd[q] * grads[q][j] for q in range(corners)) for j in range(3)]
+    sums = [sum(corner_cd[:, q, :] * grads[q][j] for q in range(corners)) for j in range(3)]
     d = [
         [sums[j][i : i + 1, :] + (1.0 if i == j else 0.0) for j in range(3)] for i in range(3)
     ]
@@ -480,7 +491,7 @@
         for ij in range(4):
             ends = []
             for k in range(2):
-                col = (2 * ij + k) * 8 + c
+                col = c * 8 + 2 * ij + k
                 value = jnp.zeros((plane, nz), f32)
                 for b in range(bz):
                     value = jnp.where(
@@ -576,7 +587,7 @@
             pltpu.VMEM((stages, 2, nx, 1, nz), f32),
             pltpu.VMEM((stages, 2, 1, nx * ny), f32),
             pltpu.VMEM((8, node_count, elem_count), bf16),
-            pltpu.VMEM((8, 8, elem_count), f32),
+            pltpu.VMEM((3, 8, elem_count), f32),
             pltpu.VMEM((blocks, slots), bf16),
             pltpu.VMEM((slots, elem_count), bf16),
             pltpu.VMEM((n, blocks), bf16),
@@ -593,10 +604,10 @@
             pltpu.SemaphoreType.DMA((3, n)),
         ],
         compiler_params=pltpu.CompilerParams(
-            collective_id=0, has_side_effects=True, vmem_limit_bytes=60 * 1024 * 1024
+            collective_id=0, has_side_effects=True, vmem_limit_bytes=20 * 1024 * 1024
         ),
         name="step",
-    )(
+    )(*(pltpu.with_memory_space_constraint(a, pltpu.HBM) for a in (
         states,
         active.transpose(1, 2, 0),
         fibre_index.transpose(1, 2, 0),
@@ -614,7 +625,7 @@
         elem_node,
         elem_fibre.reshape(1, elem_count),
         material,
-    )
+    )))
 
 
 def solution(mesh):

time: 35.5 us -> 32.9 us (0.927)
  local copies, waits for them, and re-layouts: 4.77 us -> 2.79 us
  Pallas kernels: 29.9 us -> 29.3 us
    unnamed x7 -> x3, local copies, waits for them, and re-layouts: 4.77 us -> 2.79 us
    pallas_call x1, Pallas kernels: 29.9 us -> 29.3 us  [shards(): pl.pallas_call(functools.partial(body, (mx, my, mz, seats, elem_count)),...]
where the time goes in v1:
time: 32.9 us; the launch traced here: 32.7 us
  Pallas kernels  29.3 us (89%)
  local copies, waits for them, and re-layouts  2.79 us (8%)
  between operations  0.65 us (2%)
    pallas_call x1, Pallas kernels, shards(): pl.pallas_call(functools.partial(body, (mx, my, mz, seats, elem_count)),...  29.3 us
    unnamed x3, local copies, waits for them, and re-layouts  2.79 us

profile of v1, /device:TPU:0, one launch (start us, length us, event | category | flops | bytes accessed | tf_op | source)
XLA Modules:
  0.0 32.7 jit_solution(9390226454442361468)
XLA Ops:
  0.6 29.3 %step.1 = (f32[19,16,16,128]{3,2,1,0:T(8,128)S(1)}, f32[3,16,16,128]{3,2,1,0:T(8,128)S(1)}, f32[3,512]{1,0:T(4,128)S(1)}) custom-call(f32[19,16,16,128]{3,2,1,0:T(8,128)} %states.1, s32[1,1,2]{2,1,0:T(1,128)} %bitcast.8, s32[1,1,2]{2,1,0:T(1,128)} %bitcast.9, f32[2,64]{1,0:T(2,128)} %angle_v.1, f32[2,64]{1,0:T(2,128)} %angle_v.1, f32[2,64]{1,0:T(2,128)} %conduct.1, ...), custom_call_target="tpu_custom_call" | custom-call | tf_op jit(solution)/shard_map/step/pallas_call | solution.py:572
  29.9 1.5 %copy.22 = f32[19,16,16,128]{3,2,1,0:T(8,128)} copy(f32[19,16,16,128]{3,2,1,0:T(8,128)S(1)} %get-tuple-element.6) | data formatting | bytes 4980736
  31.4 0.7 %copy.23 = f32[3,16,16,128]{3,2,1,0:T(8,128)} copy(f32[3,16,16,128]{3,2,1,0:T(8,128)S(1)} %get-tuple-element.7) | data formatting | bytes 786432
  32.1 0.6 %copy.24 = f32[3,512]{1,0:T(4,128)} copy(f32[3,512]{1,0:T(4,128)S(1)} %get-tuple-element.8) | data formatting | bytes 12288

commit v2 on v0

v2 whole, which is shorter than its diff:
```python
import functools

import jax
import jax.numpy as jnp
from jax import lax
from jax.experimental import pallas as pl
from jax.experimental.pallas import tpu as pltpu
from jax.sharding import PartitionSpec as P

NSTATE = 19
TLX = 8
SBX = 2
SBY = 2
SBZ = 32
FINE_STEPS = 2
AXES = ("gx", "gy", "gz")
MESH = pl.DeviceIdType.MESH
LANES = 128
SUB = 8
GROUPS = 4
CORNERS = 8
f32 = jnp.float32
bf16 = jnp.bfloat16
i32 = jnp.int32
calcium_keep = 0.9
tension_half = 0.09
NN = (((1,), (0,)), ((), ()))
NT = (((1,), (1,)), ((), ()))
DIRS = (
    [tuple(side if d == dim else 0 for d in range(3)) for dim in range(3) for side in (-1, 1)]
    + [(a, b, 0) for a in (-1, 1) for b in (-1, 1)]
    + [(a, 0, b) for a in (-1, 1) for b in (-1, 1)]
    + [(0, a, b) for a in (-1, 1) for b in (-1, 1)]
)
OPPOSITE = [DIRS.index(tuple(-c for c in d)) for d in DIRS]


def mm(a, b, dims=NN):
    return lax.dot_general(a, b, dims, preferred_element_type=f32)


def parts(x, count):
    out = []
    for _ in range(count):
        out.append(x.astype(bf16).astype(f32))
        x = x - out[-1]
    return out


def iota(shape, dim):
    return lax.broadcasted_iota(i32, shape, dim)


def onehot(mask):
    return jnp.where(mask, 1.0, 0.0).astype(bf16)


def pick_rows(rows, shape):
    index = iota(shape, 0)
    out = jnp.zeros(shape, f32)
    for i, row in rows.items():
        out = jnp.where(index == i, row, out)
    return out


def lane_gather(x, index):
    return jnp.take_along_axis(x, index, axis=1, mode="promise_in_bounds")


def wide(row, rows=SUB):
    return jnp.broadcast_to(row, (rows, row.shape[1]))


def gather_wide(tables, index):
    low, high = index % LANES, index // LANES
    out = lane_gather(tables[0], low)
    for h in range(1, len(tables)):
        out = jnp.where(high == h, lane_gather(tables[h], low), out)
    return out


def lane_pieces(x):
    return [x[:, h : h + LANES] for h in range(0, x.shape[1], LANES)]


def sub_sum(x):
    return jnp.sum(x, axis=0, keepdims=True)


def body(
    sizes,
    states,
    active,
    fibre_index,
    angle_s,
    angle_v,
    conduct,
    gate_half,
    gate_slope,
    gate_tau,
    conductance,
    reversal,
    ids_ref,
    weight_ref,
    node_disp,
    elem_node,
    elem_fibre,
    material,
    out,
    fine_out,
    resid_out,
    held,
    vs,
    flux,
    gate_const,
    tile_const,
    mine_coef,
    send_y,
    send_z,
    send_xy,
    send_row,
    halo_x,
    halo_y,
    halo_z,
    edge_xy,
    edge_xz,
    edge_yz,
    halo_coef,
    turned,
    slot_pos,
    inverse,
    ids_send,
    ids_got,
    val_send,
    val_got,
    ans_send,
    ans_got,
    load_sem,
    face_send_sem,
    face_recv_sem,
    coef_send_sem,
    coef_recv_sem,
    all_send_sem,
    all_recv_sem,
):
    mx, my, mz, seats, nx, ny = sizes
    nz = states.shape[3]
    n = mx * my * mz
    gates_n = NSTATE - 2
    strips = nx * ny // SUB
    bx, by, bz = nx // SBX, ny // SBY, nz // SBZ
    plane = bx * by
    blocks = plane * bz
    tiles = nx // TLX
    node_count = node_disp.shape[1]
    elem_count = elem_node.shape[1]
    rows_each = seats // GROUPS
    slots = n * rows_each
    per_group = LANES // rows_each
    slot_groups = slots // LANES
    cx, cy, cz = (lax.axis_index(a) for a in AXES)
    me = (cx * my + cy) * mz + cz
    at = (cx, cy, cz)
    counts = (mx, my, mz)

    def others():
        steps = [
            (a, b, c) for a in range(mx) for b in range(my) for c in range(mz) if a or b or c
        ]

        def far(step):
            return sum(max(s, m - s) if s else 0 for s, m in zip(step, counts))

        return sorted(steps, key=far, reverse=True)

    wrapped = [[jnp.where(p + s >= m, p + s - m, p + s) for s in range(m)] for p, m in zip(at, counts)]

    def each_other(go):
        if n <= 64:
            for step in others():
                go(tuple(wrapped[d][s] for d, s in enumerate(step)))
        else:

            def one(k, carry):
                flat = (me + k) % n
                go((flat // (my * mz), (flat // mz) % my, flat % mz))
                return carry

            lax.fori_loop(1, n, one, 0)

    for ref in (halo_x, halo_y, halo_z, edge_xy, edge_xz, edge_yz, halo_coef):
        ref[...] = jnp.zeros(ref.shape, f32)

    barrier = pltpu.get_barrier_semaphore()
    each_other(
        lambda to: pl.semaphore_signal(barrier, inc=1, device_id=to, device_id_type=MESH)
    )

    chunk = TLX * ny // SUB // 2
    loads = [
        pltpu.make_async_copy(
            states.at[:, pl.ds(i * chunk, chunk)],
            held.at[:, pl.ds(i * chunk, chunk)],
            load_sem.at[i],
        )
        for i in range(strips // chunk)
    ]
    for load in loads:
        load.start()

    def splat(value):
        return jnp.full((SUB, LANES), value, f32)

    angles = jnp.concatenate(
        [angle_v[...], jnp.zeros((2, LANES - angle_v.shape[1]), f32)], 1
    ) if angle_v.shape[1] < LANES else angle_v[...]
    rows = {0: angles[0:1], 1: angles[1:2]}
    across, spread, alive = [], [], []
    for t in range(tiles):
        index = fibre_index[0, 0, t]
        rows[2 + t] = jnp.full((1, LANES), angle_s[0, index], f32)
        rows[2 + tiles + t] = jnp.full((1, LANES), angle_s[1, index], f32)
        across.append(jnp.full((1, LANES), conduct[1, index], f32))
        spread.append(jnp.full((1, LANES), conduct[0, index], f32) - across[t])
        alive.append(jnp.where(active[0, 0, t] > 0, 1.0, 0.0).astype(f32))
    stack = pick_rows(rows, (SUB, LANES))
    cosine, sine = jnp.cos(stack), jnp.sin(stack)

    def frame_of(a, b):
        ca, sa = cosine[a : a + 1], sine[a : a + 1]
        cb, sb = cosine[b : b + 1], sine[b : b + 1]
        return ca * cb, sa * cb, sb

    for t in range(tiles):
        fx, fy, fz = frame_of(2 + t, 2 + tiles + t)
        scale = alive[t] * 0.25
        entries = [
            across[t] + spread[t] * fx * fx,
            across[t] + spread[t] * fy * fy,
            across[t] + spread[t] * fz * fz,
            spread[t] * fx * fy,
            spread[t] * fx * fz,
            spread[t] * fy * fz,
        ]
        mine_coef[t * SUB : (t + 1) * SUB] = pick_rows(
            {k: e * scale for k, e in enumerate(entries)}, (SUB, LANES)
        )

    for g in range(gates_n):
        slope = 0.5 / splat(gate_slope[g])
        gate_const[g, 0] = slope
        gate_const[g, 1] = slope * gate_half[g]
        keep = jnp.exp(-1.0 / splat(gate_tau[g]))
        share = 0.5 * (1.0 - keep)
        cond = splat(conductance[g])
        for t in range(tiles):
            live = splat(alive[t]) > 0.5
            tile_const[t, g, 0] = jnp.where(live, keep, 1.0)
            tile_const[t, g, 1] = jnp.where(live, share, 0.0)
            tile_const[t, g, 2] = jnp.where(live, cond, 0.0)
            tile_const[t, g, 3] = jnp.where(live, cond * reversal[g], 0.0)

    def live_calcium(t):
        live = splat(alive[t]) > 0.5
        keep = jnp.where(live, calcium_keep, 1.0)
        share = jnp.where(live, 0.5 * (1.0 - calcium_keep), 0.0)
        return keep, share

    def calcium_of(old, volt, t):
        keep, share = live_calcium(t)
        return old * keep + (jnp.tanh(4.0 * volt - 2.0) * share + share)

    def ionic(source, stage, i, t):
        where = pl.ds(i * chunk, chunk)
        volt = source[0, where]
        total = jnp.zeros_like(volt)
        shift = jnp.zeros_like(volt)
        for g in range(gates_n):
            bend = jnp.tanh(volt * gate_const[g, 0] - gate_const[g, 1])
            share = tile_const[t, g, 1]
            gate = source[1 + g, where] * tile_const[t, g, 0] + (bend * share + share)
            out[1 + g, where] = gate
            total = total + gate * tile_const[t, g, 2]
            shift = shift + gate * tile_const[t, g, 3]
        star = volt - (volt * total - shift)
        vs[stage, pl.ds(i * chunk * SUB, chunk * SUB)] = star.reshape(chunk * SUB, LANES)

    flat_in = (bx * bz, by)
    raw = jnp.concatenate(
        parts(ids_ref[...].astype(f32).reshape(flat_in), 3), 0
    ).astype(bf16)
    lane_b = iota((by, blocks), 1)
    put = onehot(lane_b % by == iota((by, blocks), 0))
    spread_ids = mm(raw, put)
    part = bx * bz
    spread_ids = spread_ids[:part] + spread_ids[part : 2 * part] + spread_ids[2 * part :]
    row_b, col_b = iota((part, blocks), 0), iota((part, blocks), 1)
    here = (row_b // bz == (col_b % plane) // by) & (row_b % bz == col_b // plane)
    ids = sub_sum(jnp.where(here, spread_ids, 0.0)).astype(i32)
    shift = elem_count.bit_length() - 1
    owner = lax.shift_right_logical(ids, shift)
    local = ids - owner * elem_count
    owned = onehot(owner == iota((n, blocks), 0))
    before = onehot(iota((blocks, blocks), 0) < iota((blocks, blocks), 1))
    seen = mm(owned, before)
    rank = sub_sum(owned.astype(f32) * seen).astype(i32)
    group, seat_row = rank % GROUPS, rank // GROUPS
    offset = (me % per_group) * rows_each
    hit = iota((n * GROUPS, blocks), 0) == owner * GROUPS + group
    place = onehot(iota((LANES, blocks), 0) == seat_row + offset)
    sent = jnp.concatenate(
        [
            jnp.where(hit, (local + 1).astype(f32), 0.0),
            jnp.where(hit, (iota((1, blocks), 1) + 1).astype(f32), 0.0),
        ],
        0,
    ).astype(bf16)
    sent = mm(sent, place, NT)
    ids_send[...] = sent[: n * GROUPS].reshape(n, GROUPS, LANES)
    block_at = sent[n * GROUPS :].astype(i32) - 1
    in_plane = block_at % plane
    slot_pos[...] = jnp.where(
        block_at >= 0,
        (block_at // plane // 2) * LANES
        + (in_plane // by) * ny
        + (in_plane % by) * SBY
        + (block_at // plane) % 2,
        -1,
    )
    back_row = owner * rows_each + seat_row

    raw = jnp.concatenate(parts(weight_ref[...].reshape(flat_in), 2), 0).astype(bf16)
    put = onehot(iota((by, bx * ny), 1) % ny == iota((by, bx * ny), 0) * SBY)
    spread_w = mm(raw, put)
    spread_w = (spread_w[:part] + spread_w[part:]).reshape(bx, bz, bx * ny)
    here = iota((bx, bz, bx * ny), 0) == iota((bx, bz, bx * ny), 2) // ny
    weights = jnp.sum(jnp.where(here, spread_w, 0.0), axis=0)
    weights = jnp.concatenate([weights, jnp.zeros((SUB - bz, bx * ny), f32)], 0)
    weights = weights * (1.0 / (SBX * SBY * SBZ))

    for i, load in enumerate(loads):
        load.wait()
    for t in range(tiles):

        def first(i, carry, t=t):
            ionic(held, 0, i, t)
            here = pl.ds(i * chunk, chunk)
            out[NSTATE - 1, here] = calcium_of(held[NSTATE - 1, here], held[0, here], t)
            return carry

        lax.fori_loop(2 * t, 2 * t + 2, first, 0)

    def source_of(stage, i):
        d = DIRS[i]
        if i < 2:
            return vs.at[stage, pl.ds(0 if d[0] < 0 else (nx - 2) * ny, 2 * ny)]
        if i < 4:
            return send_y.at[stage, i - 2]
        if i < 6:
            return send_z.at[stage, i - 4]
        if i < 10:
            return send_xy.at[stage, i - 6]
        return send_row.at[stage, 0 if d[2] < 0 else 1]

    def target_of(stage, i):
        if i < 2:
            return halo_x.at[stage, i]
        if i < 4:
            return halo_y.at[stage, i - 2]
        if i < 6:
            return halo_z.at[stage, i - 4]
        if i < 10:
            return edge_xy.at[stage, i - 6]
        if i < 14:
            return edge_xz.at[stage, i - 10]
        return edge_yz.at[stage, i - 14]

    def exists(i):
        ok = None
        for p, step, m in zip(at, DIRS[i], counts):
            if step:
                inside = p > 0 if step < 0 else p < m - 1
                ok = inside if ok is None else ok & inside
        return ok

    def device(i):
        return tuple(p + step for p, step in zip(at, DIRS[i]))

    order = list(range(len(DIRS) - 1, -1, -1))

    def prepare(stage):
        for side in range(2):
            for layer in range(2):
                y = layer if side == 0 else ny - 2 + layer
                send_y[stage, side, layer] = vs[stage, pl.ds(y, nx, stride=ny), :]
        for a in range(2):
            for b in range(2):
                row = (nx - 1) * a * ny + (ny - 1) * b
                send_xy[stage, 2 * a + b] = vs[stage, row : row + 1, :]
        columns = jnp.transpose(vs[stage])
        send_z[stage, 0] = columns[0:2]
        send_z[stage, 1] = columns[nz - 2 : nz]
        send_row[stage, 0] = columns[0:1]
        send_row[stage, 1] = columns[nz - 1 : nz]

    def send(stage):
        for i in order:

            @pl.when(exists(i))
            def _(i=i):
                pltpu.make_async_remote_copy(
                    src_ref=source_of(stage, i),
                    dst_ref=target_of(stage, OPPOSITE[i]),
                    send_sem=face_send_sem.at[stage, i],
                    recv_sem=face_recv_sem.at[stage, OPPOSITE[i]],
                    device_id=device(i),
                    device_id_type=MESH,
                ).start()

    def receive(stage):
        for i in range(len(DIRS)):

            @pl.when(exists(i))
            def _(i=i):
                pltpu.make_async_remote_copy(
                    src_ref=source_of(stage, i),
                    dst_ref=target_of(stage, i),
                    send_sem=face_send_sem.at[stage, i],
                    recv_sem=face_recv_sem.at[stage, i],
                    device_id=device(i),
                    device_id_type=MESH,
                ).wait()

    def coef_copy(i, landed):
        return pltpu.make_async_remote_copy(
            src_ref=mine_coef,
            dst_ref=halo_coef.at[landed],
            send_sem=coef_send_sem.at[i],
            recv_sem=coef_recv_sem.at[landed],
            device_id=device(i),
            device_id_type=MESH,
        )

    def all_start(kind, src, dst):
        dst[pl.ds(me, 1)] = src[pl.ds(me, 1)]

        def go(to):
            flat = (to[0] * my + to[1]) * mz + to[2]
            pltpu.make_async_remote_copy(
                src_ref=src.at[flat],
                dst_ref=dst.at[me],
                send_sem=all_send_sem.at[kind],
                recv_sem=all_recv_sem.at[kind],
                device_id=to,
                device_id_type=MESH,
            ).start()

        each_other(go)

    def all_wait(kind, src, dst):
        pltpu.make_async_remote_copy(
            src_ref=src.at[pl.ds(0, n - 1)],
            dst_ref=dst.at[pl.ds(0, n - 1)],
            send_sem=all_send_sem.at[kind],
            recv_sem=all_recv_sem.at[kind],
            device_id=at,
            device_id_type=MESH,
        ).wait()

    def coef_row(ref, t, k):
        return ref[t * SUB + k : t * SUB + k + 1, :]

    def diffuse(stage):
        v = vs[stage].reshape(nx, ny, nz)
        lane = iota((1, nz), 1)
        flat = nx * ny
        lane_f = iota((SUB, flat), 1)

        def both(low, high):
            return pick_rows({0: low, 1: high}, (SUB, flat))

        near = both(halo_z[stage, 0, 1:2], halo_z[stage, 1, 0:1])
        gz = both(
            send_row[stage, 0] - halo_z[stage, 0, 0:1],
            halo_z[stage, 1, 1:2] - send_row[stage, 1],
        )
        xz = [both(edge_xz[stage, 2 * a], edge_xz[stage, 2 * a + 1]) for a in range(2)]
        yz = [both(edge_yz[stage, 2 * a], edge_yz[stage, 2 * a + 1]) for a in range(2)]
        up = pltpu.roll(jnp.where(lane_f < ny, xz[1], near), flat - ny, 1)
        down = pltpu.roll(jnp.where(lane_f >= flat - ny, xz[0], near), ny, 1)
        gx = up - down
        up = jnp.where(
            lane_f % ny == ny - 1, pltpu.roll(yz[1], ny - 1, 1), pltpu.roll(near, flat - 1, 1)
        )
        down = jnp.where(
            lane_f % ny == 0, pltpu.roll(yz[0], flat - ny + 1, 1), pltpu.roll(near, 1, 1)
        )
        gy = up - down

        def coef_z(k):
            return both(
                *(
                    jnp.concatenate(
                        [coef_row(halo_coef.at[4 + s], t, k) for t in range(tiles)], 1
                    )
                    for s in range(2)
                )
            )

        fz = coef_z(4) * gx + coef_z(5) * gy + coef_z(2) * gz
        blank = jnp.zeros((SUB, flat), f32)
        half = nz // 2
        pieces = [blank] * (nz // SUB)
        pieces[0] = pick_rows(
            {0: near[0:1], **{1 + i: edge_xz[stage, i] for i in range(4)}}, (SUB, flat)
        )
        pieces[half // SUB - 1] = pick_rows({SUB - 1: fz[1:2]}, (SUB, flat))
        pieces[half // SUB] = pick_rows(
            {0: fz[0:1], **{1 + i: edge_yz[stage, i] for i in range(4)}}, (SUB, flat)
        )
        pieces[-1] = pick_rows({SUB - 1: near[1:2]}, (SUB, flat))
        turned[...] = jnp.transpose(jnp.concatenate(pieces, 0))

        def along_z(a, low, high):
            return jnp.where(lane == nz - 1, high, pltpu.roll(a, nz - 1, 1)) - jnp.where(
                lane == 0, low, pltpu.roll(a, 1, 1)
            )

        def along_rows(a, low, high):
            row = iota(a.shape, 0)
            m = a.shape[0]
            return jnp.where(row == m - 1, high, pltpu.roll(a, m - 1, 0)) - jnp.where(
                row == 0, low, pltpu.roll(a, 1, 0)
            )

        px, fx_out = [], []
        for s in range(2):
            close = halo_x[stage, s, ny:] if s == 0 else halo_x[stage, s, :ny]
            distant = halo_x[stage, s, :ny] if s == 0 else halo_x[stage, s, ny:]
            gx = v[0] - distant if s == 0 else distant - v[nx - 1]
            gy = along_rows(close, edge_xy[stage, 2 * s], edge_xy[stage, 2 * s + 1])
            first = (nx - 1) * ny if s == 0 else 0
            edge = turned[first : first + ny, :]
            c = 1 + 2 * s
            gz = along_z(close, edge[:, c : c + 1], edge[:, c + 1 : c + 2])
            t = tiles - 1 if s == 0 else 0
            k = [coef_row(halo_coef.at[s], t, j) for j in (0, 3, 4)]
            px.append(close)
            fx_out.append(k[0] * gx + k[1] * gy + k[2] * gz)
        py, fy_out = [], []
        for s in range(2):
            close, distant = halo_y[stage, s, 1 - s], halo_y[stage, s, s]
            own = vs[stage, pl.ds(0 if s == 0 else ny - 1, nx, stride=ny), :]
            gy = own - distant if s == 0 else distant - own
            gx = along_rows(close, edge_xy[stage, s], edge_xy[stage, 2 + s])
            edge = turned[pl.ds(ny - 1 if s == 0 else 0, nx, stride=ny), :]
            c = half + 1 + 2 * s
            gz = along_z(close, edge[:, c : c + 1], edge[:, c + 1 : c + 2])

            def coef_y(j, s=s):
                return jnp.concatenate(
                    [wide(coef_row(halo_coef.at[2 + s], t, j), TLX) for t in range(tiles)], 0
                )

            py.append(close)
            fy_out.append(coef_y(3) * gx + coef_y(1) * gy + coef_y(5) * gz)

        def diff_x(a, low, high):
            return jnp.concatenate([a[1:], high[None]], 0) - jnp.concatenate([low[None], a[:-1]], 0)

        def diff_y(a, low, high):
            row = iota((1, ny, nz), 1)
            up = jnp.where(row == ny - 1, high.reshape(nx, 1, nz), pltpu.roll(a, ny - 1, 1))
            down = jnp.where(row == 0, low.reshape(nx, 1, nz), pltpu.roll(a, 1, 1))
            return up - down

        def diff_z(a, edge):
            lane = iota((1, 1, nz), 2)
            up = jnp.where(lane == nz - 1, edge, pltpu.roll(a, nz - 1, 2))
            down = jnp.where(lane == 0, edge, pltpu.roll(a, 1, 2))
            return up - down

        edges = turned[...].reshape(nx, ny, nz)
        gx, gy, gz = diff_x(v, *px), diff_y(v, *py), diff_z(v, edges)
        for t in range(tiles):
            span = slice(t * TLX, (t + 1) * TLX)
            xx, yy, zz, xy, xz_, yz_ = (
                coef_row(mine_coef, t, k).reshape(1, 1, LANES) for k in range(6)
            )
            a, b, c = gx[span], gy[span], gz[span]
            flux[0, span] = xx * a + xy * b + xz_ * c
            flux[1, span] = xy * a + yy * b + yz_ * c
            flux[2, span] = xz_ * a + yz_ * b + zz * c
        edges = pltpu.roll(edges, half, 2)
        lap = (
            diff_x(flux[0], *fx_out)
            + diff_y(flux[1], *fy_out)
            + diff_z(flux[2], edges)
        )
        for t in range(tiles):
            span = slice(t * TLX, (t + 1) * TLX)
            new = v[span] + lap[span] * alive[t]
            where = pl.ds(t * TLX * ny // SUB, TLX * ny // SUB)
            out[0, where] = new.reshape(TLX * ny // SUB, SUB, LANES)

    prepare(0)
    pl.semaphore_wait(barrier, n - 1)
    send(0)
    for i in range(6):

        @pl.when(exists(i))
        def _(i=i):
            coef_copy(i, OPPOSITE[i]).start()

    all_start(0, ids_send, ids_got)

    nodes = elem_node[...]
    disp = []
    for c in range(3):
        table = [
            wide(node_disp[c : c + 1, g : g + LANES]) for g in range(0, node_count, LANES)
        ]
        disp.append([gather_wide(table, ix) for ix in lane_pieces(nodes)])
    fx, fy, fz = frame_of(0, 1)
    table = [pick_rows({0: fx, 1: fy, 2: fz}, (SUB, LANES))]
    frame8 = [gather_wide(table, wide(ix)) for ix in lane_pieces(elem_fibre[...])]
    corner = iota((CORNERS, LANES), 0)
    signs = [
        jnp.where((corner // (4 >> j)) % 2 == 1, 0.25, -0.25) for j in range(3)
    ]
    shear, bulk, scale = material[0], material[1], material[2]
    passive, pulled = [], []
    for h in range(elem_count // LANES):
        frame = [frame8[h][i : i + 1] for i in range(3)]
        d = [
            [
                sub_sum(disp[i][h] * signs[j]) + (1.0 if i == j else 0.0)
                for j in range(3)
            ]
            for i in range(3)
        ]
        cof = [
            [
                d[(i + 1) % 3][(j + 1) % 3] * d[(i + 2) % 3][(j + 2) % 3]
                - d[(i + 1) % 3][(j + 2) % 3] * d[(i + 2) % 3][(j + 1) % 3]
                for j in range(3)
            ]
            for i in range(3)
        ]
        volume = d[0][0] * cof[0][0] + d[0][1] * cof[0][1] + d[0][2] * cof[0][2]
        reciprocal = 1.0 / volume
        logv = jnp.log(volume)
        stress = [
            [
                shear * (d[i][j] - cof[i][j] * reciprocal)
                + bulk * logv * (cof[i][j] * reciprocal)
                for j in range(3)
            ]
            for i in range(3)
        ]
        stretch = [
            scale * (d[i][0] * frame[0] + d[i][1] * frame[1] + d[i][2] * frame[2])
            for i in range(3)
        ]
        along = sum(wide(frame[j]) * signs[j] for j in range(3))
        passive.append([sum(wide(stress[i][j]) * signs[j] for j in range(3)) for i in range(3)])
        pulled.append([wide(stretch[i]) * along for i in range(3)])

    found = jnp.zeros((CORNERS, node_count), f32)
    lane_e = (iota((CORNERS, elem_count), 1) + 1).astype(f32)
    for q in range(CORNERS):
        named = onehot(iota((node_count, elem_count), 0) == nodes[q : q + 1, :])
        mine = jnp.where(iota((CORNERS, elem_count), 0) == q, lane_e, 0.0).astype(bf16)
        found = found + mm(mine, named, NT)
    inverse[...] = found.astype(i32) - 1

    receive(0)
    for i in range(6):

        @pl.when(exists(i))
        def _(i=i):
            coef_copy(i, i).wait()

    diffuse(0)

    pulls = []
    for t in range(tiles):
        where = pl.ds(t * TLX * ny // SUB, TLX * ny // SUB)
        calcium = calcium_of(out[NSTATE - 1, where], out[0, where], t)
        out[NSTATE - 1, where] = calcium
        square = calcium * calcium
        pulls.append(square / (square + tension_half))
    pull = jnp.concatenate(pulls, 0).reshape(bx, SBX, ny, nz)
    pull = (pull[:, 0] + pull[:, 1]).reshape(bx * ny, nz)
    strip = onehot(iota((SUB, nz), 1) // SBZ == iota((SUB, nz), 0))
    high = pull.astype(bf16)
    rest = (pull - high.astype(f32)).astype(bf16)
    pooled = mm(strip, high, NT) + mm(strip, rest, NT)
    lanes_p = bx * ny
    value = (pooled + pltpu.roll(pooled, lanes_p - 1, 1)) * weights
    even = iota((1, lanes_p), 1) % 2 == 0
    odd_value = pltpu.roll(value, 1, 1)
    tables = [
        wide(jnp.where(even, value[b : b + 1], odd_value[b + 1 : b + 2]))
        for b in range(0, bz, 2)
    ]
    for r in range(0, n * GROUPS, SUB):
        where = slot_pos[r : r + SUB]
        picked = jnp.where(where >= 0, gather_wide(tables, jnp.maximum(where, 0)), 0.0)
        val_send[r // GROUPS : (r + SUB) // GROUPS] = picked.reshape(
            SUB // GROUPS, GROUPS, LANES
        )
    all_start(1, val_send, val_got)

    def second(t):
        def go(i, carry):
            ionic(out, 1, i, t)
            return carry

        lax.fori_loop(2 * t, 2 * t + 2, go, 0)

    second(0)

    all_wait(0, ids_send, ids_got)
    asked = []
    for g in range(slot_groups):
        total = ids_got[g * per_group]
        for m in range(1, per_group):
            total = total + ids_got[g * per_group + m]
        asked.append(total)
        index = jnp.maximum(total.astype(i32) - 1, 0)
        rows_out = []
        for k in range(GROUPS):
            where = wide(index[k : k + 1])
            rows_out += [gather_wide(disp[c], where) for c in range(3)]
            rows_out.append(jnp.zeros((SUB, LANES), f32))
        answer = jnp.transpose(jnp.concatenate(rows_out, 0))
        ans_send[g * per_group : (g + 1) * per_group] = answer.reshape(
            per_group, rows_each, LANES
        )
    all_start(2, ans_send, ans_got)
    for t in range(1, tiles):
        second(t)
    prepare(1)
    send(1)

    code = jnp.zeros((LANES, elem_count), f32)
    for g in range(slot_groups):
        column = jnp.transpose(
            jnp.concatenate([asked[g], jnp.zeros((LANES - GROUPS, LANES), f32)], 0)
        )
        ident = (iota((LANES, elem_count), 1) + 1).astype(f32)
        row = iota((LANES, elem_count), 0).astype(f32)
        for k in range(GROUPS):
            code = jnp.where(
                column[:, k : k + 1] == ident, row + float((g * GROUPS + k) * LANES), code
            )
    slot_of = sub_sum(code).astype(i32)

    all_wait(2, ans_send, ans_got)
    columns = [
        jnp.transpose(
            ans_got[g * per_group : (g + 1) * per_group].reshape(LANES, LANES)
        )
        for g in range(slot_groups)
    ]
    span = 32
    halves = []
    for h in range(blocks // LANES):
        cut = slice(h * LANES, (h + 1) * LANES)
        where, which = wide(back_row[:, cut]), wide(group[:, cut])
        rows_in = []
        for c in range(3):
            value = None
            for k in range(GROUPS):
                first = k * span + c * SUB
                found = gather_wide([col[first : first + SUB] for col in columns], where)
                value = found if value is None else jnp.where(which == k, found, value)
            value = 0.75 * value + 0.25 * pltpu.roll(value, 4, 0)
            swapped = jnp.where(
                iota((SUB, LANES), 0) // 2 % 2 == 1,
                pltpu.roll(value, 2, 0),
                pltpu.roll(value, SUB - 2, 0),
            )
            rows_in.append(0.75 * value + 0.25 * swapped)
        rows_in.append(jnp.zeros((SUB, LANES), f32))
        halves.append(jnp.concatenate(rows_in, 0))
    stacked = []
    for b in range(bz):
        lane0 = b * plane
        piece = halves[lane0 // LANES]
        stacked.append(
            pltpu.roll(piece, LANES - lane0 % LANES, 1) if lane0 % LANES else piece
        )
    around = jnp.transpose(jnp.concatenate(stacked, 0))
    lane = iota((SUB, nz), 1)
    strip_lane = lane // SBZ * span
    xi = ((lane % SBZ).astype(f32) + 0.5) / SBZ
    for p in range(bx):
        near = around[p * by : (p + 1) * by]
        for c in range(3):
            for iv in range(SBX):
                for jv in range(SBY):
                    first = c * SUB + 4 * iv + 2 * jv
                    low = lane_gather(near, strip_lane + first)
                    high = lane_gather(near, strip_lane + first + 1)
                    fine_out[c, SBX * p + iv, pl.ds(jv, by, stride=SBY), :] = (
                        low + (high - low) * xi
                    )

    receive(1)
    diffuse(1)

    all_wait(1, val_send, val_got)
    tables = []
    for g in range(slot_groups):
        total = val_got[g * per_group]
        for m in range(1, per_group):
            total = total + val_got[g * per_group + m]
        tables += [wide(total[k : k + 1]) for k in range(GROUPS)]
    tension = [gather_wide(tables, wide(ix)) for ix in lane_pieces(slot_of)]
    force = [
        [passive[h][i] + tension[h] * pulled[h][i] for h in range(elem_count // LANES)]
        for i in range(3)
    ]
    for g in range(0, node_count, LANES):
        where = inverse[:, g : g + LANES]
        index = jnp.maximum(where, 0)
        for i in range(3):
            got = jnp.where(where >= 0, gather_wide(force[i], index), 0.0)
            resid_out[i : i + 1, g : g + LANES] = sub_sum(got)


def write_out(*refs):
    count = (len(refs) - 1) // 2
    sems = refs[-1]
    copies = [
        pltpu.make_async_copy(refs[i], refs[count + i], sems.at[i]) for i in range(count)
    ]
    for c in copies:
        c.start()
    for c in copies:
        c.wait()


def shards(
    states,
    active,
    fibre_index,
    fibre_angle,
    conduct,
    gate_half,
    gate_slope,
    gate_tau,
    conductance,
    reversal,
    block_elem,
    block_weight,
    node_disp,
    elem_node,
    elem_fibre,
    material,
):
    mx, my, mz = (lax.axis_size(a) for a in AXES)
    n = mx * my * mz
    elem_count = elem_node.shape[1]
    node_count = node_disp.shape[1]
    nx, ny, nz = states.shape[1:]
    bx, by, bz = block_elem.shape
    blocks = bx * by * bz
    seats = max(2 * blocks // n, 8)
    rows_each = seats // GROUPS
    tiles = nx // TLX
    strips = nx * ny // SUB
    ids = block_elem.transpose(0, 2, 1)
    weight = block_weight.transpose(0, 2, 1)
    vmem = pl.BlockSpec(memory_space=pltpu.VMEM)
    smem = pl.BlockSpec(memory_space=pltpu.SMEM)
    hbm = pl.BlockSpec(memory_space=pltpu.HBM)
    gates_n = NSTATE - 2
    ways = len(DIRS)
    operands = (
        states.reshape(NSTATE, strips, SUB, nz),
        active.transpose(1, 2, 0),
        fibre_index.transpose(1, 2, 0),
        fibre_angle,
        fibre_angle,
        conduct,
        gate_half,
        gate_slope,
        gate_tau,
        conductance,
        reversal,
        ids,
        weight,
        node_disp,
        elem_node,
        elem_fibre.reshape(1, elem_count),
        material,
    )
    stage = FINE_STEPS
    shapes = (
        jax.ShapeDtypeStruct((NSTATE, strips, SUB, nz), f32),
        jax.ShapeDtypeStruct((3, nx, ny, nz), f32),
        jax.ShapeDtypeStruct((3, node_count), f32),
    )
    results = pl.pallas_call(
        functools.partial(body, (mx, my, mz, seats, nx, ny)),
        out_shape=shapes,
        in_specs=[hbm, smem, smem, smem, vmem] + [smem] * 6 + [vmem] * 5 + [smem],
        out_specs=(vmem, vmem, vmem),
        scratch_shapes=[
            pltpu.VMEM((NSTATE, strips, SUB, nz), f32),
            pltpu.VMEM((stage, nx * ny, nz), f32),
            pltpu.VMEM((3, nx, ny, nz), f32),
            pltpu.VMEM((gates_n, 2, SUB, LANES), f32),
            pltpu.VMEM((tiles, gates_n, 4, SUB, LANES), f32),
            pltpu.VMEM((tiles * SUB, LANES), f32),
            pltpu.VMEM((stage, 2, 2, nx, nz), f32),
            pltpu.VMEM((stage, 2, 2, nx * ny), f32),
            pltpu.VMEM((stage, 4, 1, nz), f32),
            pltpu.VMEM((stage, 2, 1, nx * ny), f32),
            pltpu.VMEM((stage, 2, 2 * ny, nz), f32),
            pltpu.VMEM((stage, 2, 2, nx, nz), f32),
            pltpu.VMEM((stage, 2, 2, nx * ny), f32),
            pltpu.VMEM((stage, 4, 1, nz), f32),
            pltpu.VMEM((stage, 4, 1, nx * ny), f32),
            pltpu.VMEM((stage, 4, 1, nx * ny), f32),
            pltpu.VMEM((6, tiles * SUB, LANES), f32),
            pltpu.VMEM((nx * ny, nz), f32),
            pltpu.VMEM((n * GROUPS, LANES), i32),
            pltpu.VMEM((CORNERS, node_count), i32),
            pltpu.VMEM((n, GROUPS, LANES), f32),
            pltpu.VMEM((n, GROUPS, LANES), f32),
            pltpu.VMEM((n, GROUPS, LANES), f32),
            pltpu.VMEM((n, GROUPS, LANES), f32),
            pltpu.VMEM((n, rows_each, LANES), f32),
            pltpu.VMEM((n, rows_each, LANES), f32),
            pltpu.SemaphoreType.DMA((2 * tiles,)),
            pltpu.SemaphoreType.DMA((stage, ways)),
            pltpu.SemaphoreType.DMA((stage, ways)),
            pltpu.SemaphoreType.DMA((6,)),
            pltpu.SemaphoreType.DMA((6,)),
            pltpu.SemaphoreType.DMA((3,)),
            pltpu.SemaphoreType.DMA((3,)),
        ],
        compiler_params=pltpu.CompilerParams(
            collective_id=0, has_side_effects=True, vmem_limit_bytes=20 * 1024 * 1024
        ),
        name="step",
    )(*(pltpu.with_memory_space_constraint(a, pltpu.HBM) for a in operands))
    results = pl.pallas_call(
        write_out,
        out_shape=shapes,
        in_specs=[vmem] * 3,
        out_specs=(hbm,) * 3,
        scratch_shapes=[pltpu.SemaphoreType.DMA((3,))],
        compiler_params=pltpu.CompilerParams(vmem_limit_bytes=20 * 1024 * 1024),
        name="write",
    )(*results)
    return results[0].reshape(states.shape), results[1], results[2]


def solution(mesh):
    in_specs = (
        P(None, "gx", "gy", "gz"),
        P("gx", "gy", "gz"),
        P("gx", "gy", "gz"),
        P(),
        P(),
        P(),
        P(),
        P(),
        P(),
        P(),
        P("gx", "gy", "gz"),
        P("gx", "gy", "gz"),
        P(None, ("gx", "gy", "gz")),
        P(None, ("gx", "gy", "gz")),
        P(("gx", "gy", "gz")),
        P(),
    )
    out_specs = (P(None, "gx", "gy", "gz"), P(None, "gx", "gy", "gz"), P(None, ("gx", "gy", "gz")))
    return jax.shard_map(shards, mesh=mesh, in_specs=in_specs, out_specs=out_specs, check_vma=False)
```

time: 35.5 us -> 22.6 us (0.64)
  Pallas kernels: 29.9 us -> 21.7 us
  local copies, waits for them, and re-layouts: 4.77 us -> 0 us
    pallas_call x1 -> x2, Pallas kernels: 29.9 us -> 21.7 us  [the longest x1 20.1 us: shards(): pl.pallas_call(functools.partial(body, (mx, my, mz, seats, nx, ny)), out_...]
    unnamed x7 -> x0, local copies, waits for them, and re-layouts: 4.77 us -> none
where the time goes in v2:
time: 22.6 us; the launch traced here: 22.4 us
  Pallas kernels  21.7 us (96%)
  between operations  0.65 us (3%)
    pallas_call x1, Pallas kernels, shards(): pl.pallas_call(functools.partial(body, (mx, my, mz, seats, nx, ny)), out_...  20.1 us
    pallas_call x1, Pallas kernels, shards(): pl.pallas_call(write_out, out_shape=shapes, in_specs=[vmem] * 3, out_spec...  1.6 us

profile of v2, /device:TPU:0, one launch (start us, length us, event | category | flops | bytes accessed | tf_op | source)
XLA Modules:
  0.0 22.4 jit_solution(11132783595762780895)
XLA Ops:
  0.6 20.1 %step.1 = (f32[19,32,8,128]{3,2,1,0:T(8,128)S(1)}, f32[3,16,16,128]{3,2,1,0:T(8,128)S(1)}, f32[3,512]{1,0:T(4,128)S(1)}) custom-call(f32[19,32,8,128]{3,2,1,0:T(8,128)} %bitcast.7, s32[1,1,2]{2,1,0:T(1,128)} %bitcast.11, s32[1,1,2]{2,1,0:T(1,128)} %bitcast.12, f32[2,64]{1,0:T(2,128)} %angle_v.1, f32[2,64]{1,0:T(2,128)} %angle_v.1, f32[2,64]{1,0:T(2,128)} %conduct.1, ...), custom_call_target="tpu_custom_call" | custom-call | tf_op jit(solution)/shard_map/step/pallas_call | solution.py:907
  20.8 1.6 %write.1 = (f32[19,32,8,128]{3,2,1,0:T(8,128)}, f32[3,16,16,128]{3,2,1,0:T(8,128)}, f32[3,512]{1,0:T(4,128)}) custom-call(f32[19,32,8,128]{3,2,1,0:T(8,128)S(1)} %get-tuple-element.9.refs_0_, f32[3,16,16,128]{3,2,1,0:T(8,128)S(1)} %get-tuple-element.10.refs_1_, f32[3,512]{1,0:T(4,128)S(1)} %get-tuple-element.11.refs_2_), custom_call_target="tpu_custom_call" | custom-call | tf_op jit(solution)/shard_map/write/pallas_call | solution.py:952

commit v3 on v2

--- a/solution.py
+++ b/solution.py
@@ -19,6 +19,7 @@
 SUB = 8
 GROUPS = 4
 CORNERS = 8
+PIECES = 4
 f32 = jnp.float32
 bf16 = jnp.bfloat16
 i32 = jnp.int32
@@ -89,61 +90,67 @@
 
 def body(
     sizes,
-    states,
-    active,
-    fibre_index,
-    angle_s,
-    angle_v,
-    conduct,
-    gate_half,
-    gate_slope,
-    gate_tau,
-    conductance,
-    reversal,
-    ids_ref,
-    weight_ref,
-    node_disp,
-    elem_node,
-    elem_fibre,
-    material,
-    out,
-    fine_out,
-    resid_out,
-    held,
-    vs,
-    flux,
-    gate_const,
-    tile_const,
-    mine_coef,
-    send_y,
-    send_z,
-    send_xy,
-    send_row,
-    halo_x,
-    halo_y,
-    halo_z,
-    edge_xy,
-    edge_xz,
-    edge_yz,
-    halo_coef,
-    turned,
-    slot_pos,
-    inverse,
-    ids_send,
-    ids_got,
-    val_send,
-    val_got,
-    ans_send,
-    ans_got,
-    load_sem,
-    face_send_sem,
-    face_recv_sem,
-    coef_send_sem,
-    coef_recv_sem,
-    all_send_sem,
-    all_recv_sem,
+    *refs,
 ):
     mx, my, mz, seats, nx, ny = sizes
+    operands, refs = refs[:17], refs[17:]
+    states = operands[0]
+    out, resid_out, answers_out, wanted_out = refs[:4]
+    small, refs = refs[4:20], refs[20:]
+    (
+        active,
+        fibre_index,
+        angle_s,
+        angle_v,
+        conduct,
+        gate_half,
+        gate_slope,
+        gate_tau,
+        conductance,
+        reversal,
+        ids_ref,
+        weight_ref,
+        node_disp,
+        elem_node,
+        elem_fibre,
+        material,
+    ) = small
+    (
+        held,
+        vs,
+        flux,
+        gate_const,
+        tile_const,
+        mine_coef,
+        send_y,
+        send_z,
+        send_xy,
+        send_row,
+        halo_x,
+        halo_y,
+        halo_z,
+        edge_xy,
+        edge_xz,
+        edge_yz,
+        halo_coef,
+        turned,
+        slot_pos,
+        inverse,
+        ids_send,
+        ids_got,
+        val_send,
+        val_got,
+        ans_send,
+        ans_got,
+        load_sem,
+        small_sem,
+        face_send_sem,
+        face_recv_sem,
+        coef_send_sem,
+        coef_recv_sem,
+        all_send_sem,
+        all_recv_sem,
+    ) = refs
     nz = states.shape[3]
     n = mx * my * mz
     gates_n = NSTATE - 2
@@ -188,6 +195,21 @@
 
             lax.fori_loop(1, n, one, 0)
 
+    chunk = TLX * ny // SUB // 2
+
+    def load(i):
+        here = pl.ds(i * chunk, chunk)
+        return pltpu.make_async_copy(states.at[:, here], held.at[:, here], load_sem.at[i])
+
+    small_loads = [
+        pltpu.make_async_copy(src, dst, small_sem.at[i])
+        for i, (src, dst) in enumerate(zip(operands[1:], small))
+    ]
+    for c in small_loads:
+        c.start()
+    for i in range(strips // chunk):
+        load(i).start()
+
     for ref in (halo_x, halo_y, halo_z, edge_xy, edge_xz, edge_yz, halo_coef):
         ref[...] = jnp.zeros(ref.shape, f32)
 
@@ -196,17 +218,8 @@
         lambda to: pl.semaphore_signal(barrier, inc=1, device_id=to, device_id_type=MESH)
     )
 
-    chunk = TLX * ny // SUB // 2
-    loads = [
-        pltpu.make_async_copy(
-            states.at[:, pl.ds(i * chunk, chunk)],
-            held.at[:, pl.ds(i * chunk, chunk)],
-            load_sem.at[i],
-        )
-        for i in range(strips // chunk)
-    ]
-    for load in loads:
-        load.start()
+    for c in small_loads:
+        c.wait()
 
     def splat(value):
         return jnp.full((SUB, LANES), value, f32)
@@ -338,11 +351,10 @@
     weights = jnp.concatenate([weights, jnp.zeros((SUB - bz, bx * ny), f32)], 0)
     weights = weights * (1.0 / (SBX * SBY * SBZ))
 
-    for i, load in enumerate(loads):
-        load.wait()
     for t in range(tiles):
 
         def first(i, carry, t=t):
+            load(i).wait()
             ionic(held, 0, i, t)
             here = pl.ds(i * chunk, chunk)
             out[NSTATE - 1, here] = calcium_of(held[NSTATE - 1, here], held[0, here], t)
@@ -605,6 +617,7 @@
 
     prepare(0)
     pl.semaphore_wait(barrier, n - 1)
+    all_start(0, ids_send, ids_got)
     send(0)
     for i in range(6):
 
@@ -612,7 +625,6 @@
         def _(i=i):
             coef_copy(i, OPPOSITE[i]).start()
 
-    all_start(0, ids_send, ids_got)
 
     nodes = elem_node[...]
     disp = []
@@ -719,8 +731,6 @@
 
         lax.fori_loop(2 * t, 2 * t + 2, go, 0)
 
-    second(0)
-
     all_wait(0, ids_send, ids_got)
     asked = []
     for g in range(slot_groups):
@@ -739,7 +749,7 @@
             per_group, rows_each, LANES
         )
     all_start(2, ans_send, ans_got)
-    for t in range(1, tiles):
+    for t in range(tiles):
         second(t)
     prepare(1)
     send(1)
@@ -757,10 +767,56 @@
             )
     slot_of = sub_sum(code).astype(i32)
 
+    receive(1)
+    diffuse(1)
+
+    all_wait(1, val_send, val_got)
+    tables = []
+    for g in range(slot_groups):
+        total = val_got[g * per_group]
+        for m in range(1, per_group):
+            total = total + val_got[g * per_group + m]
+        tables += [wide(total[k : k + 1]) for k in range(GROUPS)]
+    tension = [gather_wide(tables, wide(ix)) for ix in lane_pieces(slot_of)]
+    force = [
+        [passive[h][i] + tension[h] * pulled[h][i] for h in range(elem_count // LANES)]
+        for i in range(3)
+    ]
+    for g in range(0, node_count, LANES):
+        where = inverse[:, g : g + LANES]
+        index = jnp.maximum(where, 0)
+        for i in range(3):
+            got = jnp.where(where >= 0, gather_wide(force[i], index), 0.0)
+            resid_out[i : i + 1, g : g + LANES] = sub_sum(got)
+
+    wanted_out[0:1] = back_row
+    wanted_out[1:2] = group
     all_wait(2, ans_send, ans_got)
+    answers_out[...] = ans_got[...]
+
+
+def write_out(states, resid, answers, wanted, states_out, fine_out, resid_out, fine, sems):
+    n, rows_each = answers.shape[:2]
+    nx, ny, nz = fine.shape[1:]
+    bx, by, bz = nx // SBX, ny // SBY, nz // SBZ
+    plane = bx * by
+    blocks = plane * bz
+    per_group = LANES // rows_each
+    slot_groups = n * rows_each // LANES
+    copies = [
+        pltpu.make_async_copy(states, states_out, sems.at[0]),
+        pltpu.make_async_copy(resid, resid_out, sems.at[1]),
+    ]
+    for c in copies:
+        c.start()
+
+    def fine_copy(i):
+        here = pl.ds(i * nx // PIECES, nx // PIECES)
+        return pltpu.make_async_copy(fine.at[:, here], fine_out.at[:, here], sems.at[2 + i])
+
     columns = [
         jnp.transpose(
-            ans_got[g * per_group : (g + 1) * per_group].reshape(LANES, LANES)
+            answers[g * per_group : (g + 1) * per_group].reshape(LANES, LANES)
         )
         for g in range(slot_groups)
     ]
@@ -768,7 +824,7 @@
     halves = []
     for h in range(blocks // LANES):
         cut = slice(h * LANES, (h + 1) * LANES)
-        where, which = wide(back_row[:, cut]), wide(group[:, cut])
+        where, which = wide(wanted[0:1, cut]), wide(wanted[1:2, cut])
         rows_in = []
         for c in range(3):
             value = None
@@ -804,41 +860,13 @@
                     first = c * SUB + 4 * iv + 2 * jv
                     low = lane_gather(near, strip_lane + first)
                     high = lane_gather(near, strip_lane + first + 1)
-                    fine_out[c, SBX * p + iv, pl.ds(jv, by, stride=SBY), :] = (
+                    fine[c, SBX * p + iv, pl.ds(jv, by, stride=SBY), :] = (
                         low + (high - low) * xi
                     )
-
-    receive(1)
-    diffuse(1)
-
-    all_wait(1, val_send, val_got)
-    tables = []
-    for g in range(slot_groups):
-        total = val_got[g * per_group]
-        for m in range(1, per_group):
-            total = total + val_got[g * per_group + m]
-        tables += [wide(total[k : k + 1]) for k in range(GROUPS)]
-    tension = [gather_wide(tables, wide(ix)) for ix in lane_pieces(slot_of)]
-    force = [
-        [passive[h][i] + tension[h] * pulled[h][i] for h in range(elem_count // LANES)]
-        for i in range(3)
-    ]
-    for g in range(0, node_count, LANES):
-        where = inverse[:, g : g + LANES]
-        index = jnp.maximum(where, 0)
-        for i in range(3):
-            got = jnp.where(where >= 0, gather_wide(force[i], index), 0.0)
-            resid_out[i : i + 1, g : g + LANES] = sub_sum(got)
-
-
-def write_out(*refs):
-    count = (len(refs) - 1) // 2
-    sems = refs[-1]
-    copies = [
-        pltpu.make_async_copy(refs[i], refs[count + i], sems.at[i]) for i in range(count)
-    ]
-    for c in copies:
-        c.start()
+        if (p + 1) % (bx // PIECES) == 0:
+            fine_copy(p // (bx // PIECES)).start()
+    for i in range(PIECES):
+        fine_copy(i).wait()
     for c in copies:
         c.wait()
 
@@ -875,7 +903,6 @@
     ids = block_elem.transpose(0, 2, 1)
     weight = block_weight.transpose(0, 2, 1)
     vmem = pl.BlockSpec(memory_space=pltpu.VMEM)
-    smem = pl.BlockSpec(memory_space=pltpu.SMEM)
     hbm = pl.BlockSpec(memory_space=pltpu.HBM)
     gates_n = NSTATE - 2
     ways = len(DIRS)
@@ -899,17 +926,25 @@
         material,
     )
     stage = FINE_STEPS
-    shapes = (
-        jax.ShapeDtypeStruct((NSTATE, strips, SUB, nz), f32),
-        jax.ShapeDtypeStruct((3, nx, ny, nz), f32),
-        jax.ShapeDtypeStruct((3, node_count), f32),
-    )
+    states_shape = jax.ShapeDtypeStruct((NSTATE, strips, SUB, nz), f32)
+    fine_shape = jax.ShapeDtypeStruct((3, nx, ny, nz), f32)
+    resid_shape = jax.ShapeDtypeStruct((3, node_count), f32)
+    in_smem = [True] * 3 + [False] + [True] * 6 + [False] * 5 + [True]
     results = pl.pallas_call(
         functools.partial(body, (mx, my, mz, seats, nx, ny)),
-        out_shape=shapes,
-        in_specs=[hbm, smem, smem, smem, vmem] + [smem] * 6 + [vmem] * 5 + [smem],
-        out_specs=(vmem, vmem, vmem),
+        out_shape=(
+            states_shape,
+            resid_shape,
+            jax.ShapeDtypeStruct((n, rows_each, LANES), f32),
+            jax.ShapeDtypeStruct((2, blocks), i32),
+        ),
+        in_specs=[hbm] * len(operands),
+        out_specs=(vmem,) * 4,
         scratch_shapes=[
+            (pltpu.SMEM if scalar else pltpu.VMEM)(x.shape, x.dtype)
+            for scalar, x in zip(in_smem, operands[1:])
+        ]
+        + [
             pltpu.VMEM((NSTATE, strips, SUB, nz), f32),
             pltpu.VMEM((stage, nx * ny, nz), f32),
             pltpu.VMEM((3, nx, ny, nz), f32),
@@ -937,6 +972,7 @@
             pltpu.VMEM((n, rows_each, LANES), f32),
             pltpu.VMEM((n, rows_each, LANES), f32),
             pltpu.SemaphoreType.DMA((2 * tiles,)),
+            pltpu.SemaphoreType.DMA((len(operands) - 1,)),
             pltpu.SemaphoreType.DMA((stage, ways)),
             pltpu.SemaphoreType.DMA((stage, ways)),
             pltpu.SemaphoreType.DMA((6,)),
@@ -951,10 +987,13 @@
     )(*(pltpu.with_memory_space_constraint(a, pltpu.HBM) for a in operands))
     results = pl.pallas_call(
         write_out,
-        out_shape=shapes,
-        in_specs=[vmem] * 3,
+        out_shape=(states_shape, fine_shape, resid_shape),
+        in_specs=[vmem] * 4,
         out_specs=(hbm,) * 3,
-        scratch_shapes=[pltpu.SemaphoreType.DMA((3,))],
+        scratch_shapes=[
+            pltpu.VMEM((3, nx, ny, nz), f32),
+            pltpu.SemaphoreType.DMA((2 + PIECES,)),
+        ],
         compiler_params=pltpu.CompilerParams(vmem_limit_bytes=20 * 1024 * 1024),
         name="write",
     )(*results)

time: 22.6 us -> 20.5 us (0.907)
  Pallas kernels: 21.7 us -> 19.8 us
    pallas_call x1, Pallas kernels: 20.1 us -> 18.1 us  [shards(): pl.pallas_call(functools.partial(body, (mx, my, mz, seats, nx, ny)), out_...]
where the time goes in v3:
time: 20.5 us; the launch traced here: 20.4 us
  Pallas kernels  19.8 us (97%)
  between operations  0.65 us (3%)
    pallas_call x1, Pallas kernels, shards(): pl.pallas_call(functools.partial(body, (mx, my, mz, seats, nx, ny)), out_...  18.1 us
    pallas_call x1, Pallas kernels, shards(): pl.pallas_call(write_out, out_shape=(states_shape, fine_shape, resid_shap...  1.62 us

profile of v3, /device:TPU:0, one launch (start us, length us, event | category | flops | bytes accessed | tf_op | source)
XLA Modules:
  0.0 20.4 jit_solution(11786237184983938643)
XLA Ops:
  0.6 18.1 %step.1 = (f32[19,32,8,128]{3,2,1,0:T(8,128)S(1)}, f32[3,512]{1,0:T(4,128)S(1)}, f32[32,4,128]{2,1,0:T(4,128)S(1)}, s32[2,256]{1,0:T(2,128)S(1)}) custom-call(f32[19,32,8,128]{3,2,1,0:T(8,128)} %bitcast.7, s32[1,1,2]{2,1,0:T(1,128)} %bitcast.11, s32[1,1,2]{2,1,0:T(1,128)} %bitcast.12, f32[2,64]{1,0:T(2,128)} %refs_4_.1, f32[2,64]{1,0:T(2,128)} %refs_4_.1, ...), custom_call_target="tpu_custom_call" | custom-call | tf_op jit(solution)/shard_map/step/pallas_call | solution.py:933
  18.8 1.6 %write.1 = (f32[19,32,8,128]{3,2,1,0:T(8,128)}, f32[3,16,16,128]{3,2,1,0:T(8,128)}, f32[3,512]{1,0:T(4,128)}) custom-call(f32[19,32,8,128]{3,2,1,0:T(8,128)S(1)} %get-tuple-element.10.states, f32[3,512]{1,0:T(4,128)S(1)} %get-tuple-element.11.resid, f32[32,4,128]{2,1,0:T(4,128)S(1)} %get-tuple-element.12.answers, s32[2,256]{1,0:T(2,128)S(1)} %get-tuple-element.13.wanted), custom_call_target="tpu_custom_call" | custom-call | tf_op jit(solution)/shard_map/write/pallas_call | solution.py:988

commit v4 on v3

--- a/solution.py
+++ b/solution.py
@@ -17,8 +17,8 @@
 MESH = pl.DeviceIdType.MESH
 LANES = 128
 SUB = 8
-GROUPS = 4
 CORNERS = 8
+ROWS = 4
 PIECES = 4
 f32 = jnp.float32
 bf16 = jnp.bfloat16
@@ -84,6 +84,16 @@
     return [x[:, h : h + LANES] for h in range(0, x.shape[1], LANES)]
 
 
+def row_totals(got, per_row, row):
+    totals = []
+    for r in range(0, got.shape[0], per_row):
+        total = got[r, row : row + 1]
+        for m in range(1, per_row):
+            total = total + got[r + m, row : row + 1]
+        totals.append(total)
+    return totals
+
+
 def sub_sum(x):
     return jnp.sum(x, axis=0, keepdims=True)
 
@@ -95,8 +105,8 @@
     mx, my, mz, seats, nx, ny = sizes
     operands, refs = refs[:17], refs[17:]
     states = operands[0]
-    out, resid_out, answers_out, wanted_out = refs[:4]
-    small, refs = refs[4:20], refs[20:]
+    out, answers_out, wanted_out, inverse, forces_out = refs[:5]
+    small, refs = refs[5:21], refs[21:]
     (
         active,
         fibre_index,
@@ -121,6 +131,8 @@
         flux,
         gate_const,
         tile_const,
+        sums,
+        bends,
         mine_coef,
         send_y,
         send_z,
@@ -133,13 +145,11 @@
         edge_xz,
         edge_yz,
         halo_coef,
+        tally,
         turned,
         slot_pos,
-        inverse,
         ids_send,
         ids_got,
-        val_send,
-        val_got,
         ans_send,
         ans_got,
         load_sem,
@@ -161,10 +171,10 @@
     tiles = nx // TLX
     node_count = node_disp.shape[1]
     elem_count = elem_node.shape[1]
-    rows_each = seats // GROUPS
-    slots = n * rows_each
-    per_group = LANES // rows_each
-    slot_groups = slots // LANES
+    per_group = LANES // ROWS
+    slot_groups = n // per_group
+    per_row = LANES // seats
+    slot_rows = n // per_row
     cx, cy, cz = (lax.axis_index(a) for a in AXES)
     me = (cx * my + cy) * mz + cz
     at = (cx, cy, cz)
@@ -176,7 +186,10 @@
         ]
 
         def far(step):
-            return sum(max(s, m - s) if s else 0 for s, m in zip(step, counts))
+            return sum(
+                (1 if d == 1 else max(s, m - s)) if s else 0
+                for d, (s, m) in enumerate(zip(step, counts))
+            )
 
         return sorted(steps, key=far, reverse=True)
 
@@ -210,8 +223,10 @@
     for i in range(strips // chunk):
         load(i).start()
 
-    for ref in (halo_x, halo_y, halo_z, edge_xy, edge_xz, edge_yz, halo_coef):
-        ref[...] = jnp.zeros(ref.shape, f32)
+    for ref in (halo_x, halo_y, halo_z, edge_xy, edge_xz, edge_yz):
+        used = ref.shape[1] // 2
+        ref[:, :used] = jnp.zeros((ref.shape[0], used) + ref.shape[2:], f32)
+    halo_coef[:6] = jnp.zeros((6,) + halo_coef.shape[1:], f32)
 
     barrier = pltpu.get_barrier_semaphore()
     each_other(
@@ -271,7 +286,10 @@
             tile_const[t, g, 0] = jnp.where(live, keep, 1.0)
             tile_const[t, g, 1] = jnp.where(live, share, 0.0)
             tile_const[t, g, 2] = jnp.where(live, cond, 0.0)
-            tile_const[t, g, 3] = jnp.where(live, cond * reversal[g], 0.0)
+            pull = cond * reversal[g]
+            tile_const[t, g, 3] = jnp.where(live, pull, 0.0)
+            tile_const[t, g, 4] = jnp.where(live, cond * share, 0.0)
+            tile_const[t, g, 5] = jnp.where(live, pull * share, 0.0)
 
     def live_calcium(t):
         live = splat(alive[t]) > 0.5
@@ -283,20 +301,59 @@
         keep, share = live_calcium(t)
         return old * keep + (jnp.tanh(4.0 * volt - 2.0) * share + share)
 
-    def ionic(source, stage, i, t):
+    def ionic(i, t):
         where = pl.ds(i * chunk, chunk)
-        volt = source[0, where]
+        volt = held[0, where]
         total = jnp.zeros_like(volt)
         shift = jnp.zeros_like(volt)
         for g in range(gates_n):
             bend = jnp.tanh(volt * gate_const[g, 0] - gate_const[g, 1])
             share = tile_const[t, g, 1]
-            gate = source[1 + g, where] * tile_const[t, g, 0] + (bend * share + share)
+            gate = held[1 + g, where] * tile_const[t, g, 0] + (bend * share + share)
             out[1 + g, where] = gate
             total = total + gate * tile_const[t, g, 2]
             shift = shift + gate * tile_const[t, g, 3]
         star = volt - (volt * total - shift)
-        vs[stage, pl.ds(i * chunk * SUB, chunk * SUB)] = star.reshape(chunk * SUB, LANES)
+        vs[0, pl.ds(i * chunk * SUB, chunk * SUB)] = star.reshape(chunk * SUB, LANES)
+
+    def ionic_before(i, t):
+        where = pl.ds(i * chunk, chunk)
+        total = jnp.zeros((chunk, SUB, LANES), f32)
+        shift = jnp.zeros((chunk, SUB, LANES), f32)
+        for g in range(gates_n):
+            kept = out[1 + g, where] * tile_const[t, g, 0] + tile_const[t, g, 1]
+            out[1 + g, where] = kept
+            total = total + kept * tile_const[t, g, 2]
+            shift = shift + kept * tile_const[t, g, 3]
+        sums[0, where] = total
+        sums[1, where] = shift
+
+    def ionic_between(i, t):
+        where = pl.ds(i * chunk, chunk)
+        volt = out[0, where]
+        total = sums[0, where]
+        shift = sums[1, where]
+        for g in range(gates_n):
+            bend = jnp.tanh(volt * gate_const[g, 0] - gate_const[g, 1])
+            bends[g, where] = bend
+            total = total + bend * tile_const[t, g, 4]
+            shift = shift + bend * tile_const[t, g, 5]
+        star = volt - (volt * total - shift)
+        vs[1, pl.ds(i * chunk * SUB, chunk * SUB)] = star.reshape(chunk * SUB, LANES)
+
+    def ionic_after(i, t):
+        where = pl.ds(i * chunk, chunk)
+        for g in range(gates_n):
+            out[1 + g, where] = out[1 + g, where] + bends[g, where] * tile_const[t, g, 1]
+
+    def over_chunks(step):
+        for t in range(tiles):
+
+            def go(i, carry, t=t):
+                step(i, t)
+                return carry
+
+            lax.fori_loop(2 * t, 2 * t + 2, go, 0)
 
     flat_in = (bx * bz, by)
     raw = jnp.concatenate(
@@ -317,10 +374,9 @@
     before = onehot(iota((blocks, blocks), 0) < iota((blocks, blocks), 1))
     seen = mm(owned, before)
     rank = sub_sum(owned.astype(f32) * seen).astype(i32)
-    group, seat_row = rank % GROUPS, rank // GROUPS
-    offset = (me % per_group) * rows_each
-    hit = iota((n * GROUPS, blocks), 0) == owner * GROUPS + group
-    place = onehot(iota((LANES, blocks), 0) == seat_row + offset)
+    offset = (me % per_row) * seats
+    hit = owner == iota((n, blocks), 0)
+    place = onehot(iota((LANES, blocks), 0) == rank + offset)
     sent = jnp.concatenate(
         [
             jnp.where(hit, (local + 1).astype(f32), 0.0),
@@ -329,8 +385,8 @@
         0,
     ).astype(bf16)
     sent = mm(sent, place, NT)
-    ids_send[...] = sent[: n * GROUPS].reshape(n, GROUPS, LANES)
-    block_at = sent[n * GROUPS :].astype(i32) - 1
+    ids_send[...] = sent[:n].reshape(n, 1, LANES)
+    block_at = sent[n:].astype(i32) - 1
     in_plane = block_at % plane
     slot_pos[...] = jnp.where(
         block_at >= 0,
@@ -340,7 +396,8 @@
         + (block_at // plane) % 2,
         -1,
     )
-    back_row = owner * rows_each + seat_row
+    wanted_out[0:1] = owner
+    wanted_out[1:2] = rank
 
     raw = jnp.concatenate(parts(weight_ref[...].reshape(flat_in), 2), 0).astype(bf16)
     put = onehot(iota((by, bx * ny), 1) % ny == iota((by, bx * ny), 0) * SBY)
@@ -351,16 +408,13 @@
     weights = jnp.concatenate([weights, jnp.zeros((SUB - bz, bx * ny), f32)], 0)
     weights = weights * (1.0 / (SBX * SBY * SBZ))
 
-    for t in range(tiles):
-
-        def first(i, carry, t=t):
-            load(i).wait()
-            ionic(held, 0, i, t)
-            here = pl.ds(i * chunk, chunk)
-            out[NSTATE - 1, here] = calcium_of(held[NSTATE - 1, here], held[0, here], t)
-            return carry
-
-        lax.fori_loop(2 * t, 2 * t + 2, first, 0)
+    def first(i, t):
+        load(i).wait()
+        ionic(i, t)
+        here = pl.ds(i * chunk, chunk)
+        out[NSTATE - 1, here] = calcium_of(held[NSTATE - 1, here], held[0, here], t)
+
+    over_chunks(first)
 
     def source_of(stage, i):
         d = DIRS[i]
@@ -374,18 +428,10 @@
             return send_xy.at[stage, i - 6]
         return send_row.at[stage, 0 if d[2] < 0 else 1]
 
-    def target_of(stage, i):
-        if i < 2:
-            return halo_x.at[stage, i]
-        if i < 4:
-            return halo_y.at[stage, i - 2]
-        if i < 6:
-            return halo_z.at[stage, i - 4]
-        if i < 10:
-            return edge_xy.at[stage, i - 6]
-        if i < 14:
-            return edge_xz.at[stage, i - 10]
-        return edge_yz.at[stage, i - 14]
+    families = (
+        [(halo_x, 0, 2), (halo_y, 2, 2), (halo_z, 4, 2)]
+        + [(edge_xy, 6, 4), (edge_xz, 10, 4), (edge_yz, 14, 4)]
+    )
 
     def exists(i):
         ok = None
@@ -395,8 +441,17 @@
                 ok = inside if ok is None else ok & inside
         return ok
 
-    def device(i):
-        return tuple(p + step for p, step in zip(at, DIRS[i]))
+    def route(i):
+        ok = exists(i)
+        swap = next(d for d in (1, 0, 2) if DIRS[i][d] == 0)
+        to = []
+        for d, (p, step) in enumerate(zip(at, DIRS[i])):
+            if step:
+                p = jnp.where(ok, p + step, p)
+            elif d == swap:
+                p = jnp.where(ok, p, p + 1 - 2 * (p % 2))
+            to.append(p)
+        return tuple(to), ok
 
     order = list(range(len(DIRS) - 1, -1, -1))
 
@@ -417,41 +472,49 @@
 
     def send(stage):
         for i in order:
-
-            @pl.when(exists(i))
-            def _(i=i):
-                pltpu.make_async_remote_copy(
-                    src_ref=source_of(stage, i),
-                    dst_ref=target_of(stage, OPPOSITE[i]),
-                    send_sem=face_send_sem.at[stage, i],
-                    recv_sem=face_recv_sem.at[stage, OPPOSITE[i]],
-                    device_id=device(i),
-                    device_id_type=MESH,
-                ).start()
+            ref, first, count = next(f for f in families if f[1] <= i < f[1] + f[2])
+            to, ok = route(i)
+            slot = jnp.where(ok, OPPOSITE[i] - first, count + i - first)
+            pltpu.make_async_remote_copy(
+                src_ref=source_of(stage, i),
+                dst_ref=ref.at[stage, slot],
+                send_sem=face_send_sem.at[stage],
+                recv_sem=face_recv_sem.at[stage],
+                device_id=to,
+                device_id_type=MESH,
+            ).start()
 
     def receive(stage):
-        for i in range(len(DIRS)):
-
-            @pl.when(exists(i))
-            def _(i=i):
-                pltpu.make_async_remote_copy(
-                    src_ref=source_of(stage, i),
-                    dst_ref=target_of(stage, i),
-                    send_sem=face_send_sem.at[stage, i],
-                    recv_sem=face_recv_sem.at[stage, i],
-                    device_id=device(i),
-                    device_id_type=MESH,
-                ).wait()
-
-    def coef_copy(i, landed):
-        return pltpu.make_async_remote_copy(
-            src_ref=mine_coef,
-            dst_ref=halo_coef.at[landed],
-            send_sem=coef_send_sem.at[i],
-            recv_sem=coef_recv_sem.at[landed],
-            device_id=device(i),
+        pltpu.make_async_remote_copy(
+            src_ref=tally,
+            dst_ref=tally,
+            send_sem=face_send_sem.at[stage],
+            recv_sem=face_recv_sem.at[stage],
+            device_id=at,
             device_id_type=MESH,
-        )
+        ).wait()
+
+    def send_coef():
+        for i in range(6):
+            to, ok = route(i)
+            pltpu.make_async_remote_copy(
+                src_ref=mine_coef,
+                dst_ref=halo_coef.at[jnp.where(ok, OPPOSITE[i], 6 + i)],
+                send_sem=coef_send_sem,
+                recv_sem=coef_recv_sem,
+                device_id=to,
+                device_id_type=MESH,
+            ).start()
+
+    def receive_coef():
+        pltpu.make_async_remote_copy(
+            src_ref=halo_coef.at[pl.ds(0, 6)],
+            dst_ref=halo_coef.at[pl.ds(0, 6)],
+            send_sem=coef_send_sem,
+            recv_sem=coef_recv_sem,
+            device_id=at,
+            device_id_type=MESH,
+        ).wait()
 
     def all_start(kind, src, dst):
         dst[pl.ds(me, 1)] = src[pl.ds(me, 1)]
@@ -619,13 +682,10 @@
     pl.semaphore_wait(barrier, n - 1)
     all_start(0, ids_send, ids_got)
     send(0)
-    for i in range(6):
-
-        @pl.when(exists(i))
-        def _(i=i):
-            coef_copy(i, OPPOSITE[i]).start()
-
-
+    send_coef()
+
+
+    over_chunks(ionic_before)
     nodes = elem_node[...]
     disp = []
     for c in range(3):
@@ -641,7 +701,6 @@
         jnp.where((corner // (4 >> j)) % 2 == 1, 0.25, -0.25) for j in range(3)
     ]
     shear, bulk, scale = material[0], material[1], material[2]
-    passive, pulled = [], []
     for h in range(elem_count // LANES):
         frame = [frame8[h][i : i + 1] for i in range(3)]
         d = [
@@ -675,8 +734,10 @@
             for i in range(3)
         ]
         along = sum(wide(frame[j]) * signs[j] for j in range(3))
-        passive.append([sum(wide(stress[i][j]) * signs[j] for j in range(3)) for i in range(3)])
-        pulled.append([wide(stretch[i]) * along for i in range(3)])
+        cut = slice(h * LANES, (h + 1) * LANES)
+        for i in range(3):
+            forces_out[i, :, cut] = sum(wide(stress[i][j]) * signs[j] for j in range(3))
+            forces_out[3 + i, :, cut] = wide(stretch[i]) * along
 
     found = jnp.zeros((CORNERS, node_count), f32)
     lane_e = (iota((CORNERS, elem_count), 1) + 1).astype(f32)
@@ -687,12 +748,7 @@
     inverse[...] = found.astype(i32) - 1
 
     receive(0)
-    for i in range(6):
-
-        @pl.when(exists(i))
-        def _(i=i):
-            coef_copy(i, i).wait()
-
+    receive_coef()
     diffuse(0)
 
     pulls = []
@@ -716,122 +772,135 @@
         wide(jnp.where(even, value[b : b + 1], odd_value[b + 1 : b + 2]))
         for b in range(0, bz, 2)
     ]
-    for r in range(0, n * GROUPS, SUB):
+    value_rows = []
+    for r in range(0, n, SUB):
         where = slot_pos[r : r + SUB]
-        picked = jnp.where(where >= 0, gather_wide(tables, jnp.maximum(where, 0)), 0.0)
-        val_send[r // GROUPS : (r + SUB) // GROUPS] = picked.reshape(
-            SUB // GROUPS, GROUPS, LANES
+        value_rows.append(
+            jnp.where(where >= 0, gather_wide(tables, jnp.maximum(where, 0)), 0.0)
         )
-    all_start(1, val_send, val_got)
-
-    def second(t):
-        def go(i, carry):
-            ionic(out, 1, i, t)
-            return carry
-
-        lax.fori_loop(2 * t, 2 * t + 2, go, 0)
 
     all_wait(0, ids_send, ids_got)
-    asked = []
+    asked = row_totals(ids_got, per_row, 0)
+    asked_wide = [wide(row) for row in asked]
+    place = iota((SUB, LANES), 1)
+    which = place % ROWS
     for g in range(slot_groups):
-        total = ids_got[g * per_group]
-        for m in range(1, per_group):
-            total = total + ids_got[g * per_group + m]
-        asked.append(total)
-        index = jnp.maximum(total.astype(i32) - 1, 0)
+        device_at = g * per_group + place // ROWS
         rows_out = []
-        for k in range(GROUPS):
-            where = wide(index[k : k + 1])
-            rows_out += [gather_wide(disp[c], where) for c in range(3)]
-            rows_out.append(jnp.zeros((SUB, LANES), f32))
+        for seat in range(seats):
+            source = (device_at % per_row) * seats + seat
+            where = None
+            for r in range(g * per_group // per_row, -(-(g + 1) * per_group // per_row)):
+                found = lane_gather(asked_wide[r], source)
+                where = (
+                    found if where is None else jnp.where(device_at // per_row == r, found, where)
+                )
+            where = jnp.maximum(where.astype(i32) - 1, 0)
+            low, high = where % LANES, where // LANES
+            value = None
+            for c in range(3):
+                for h in range(elem_count // LANES):
+                    found = lane_gather(disp[c][h], low)
+                    value = (
+                        found
+                        if value is None
+                        else jnp.where((which == c) & (high == h), found, value)
+                    )
+            rows_out.append(value)
+        rows_out += [jnp.zeros((SUB, LANES), f32)] * (LANES // SUB - seats)
         answer = jnp.transpose(jnp.concatenate(rows_out, 0))
-        ans_send[g * per_group : (g + 1) * per_group] = answer.reshape(
-            per_group, rows_each, LANES
-        )
-    all_start(2, ans_send, ans_got)
-    for t in range(tiles):
-        second(t)
+        ans_send[g * per_group : (g + 1) * per_group] = answer.reshape(per_group, ROWS, LANES)
+    for r in range(0, n, SUB):
+        ans_send[r : r + SUB, 3:4] = value_rows[r // SUB].reshape(SUB, 1, LANES)
+    all_start(1, ans_send, ans_got)
+    over_chunks(ionic_between)
     prepare(1)
     send(1)
+    over_chunks(ionic_after)
 
     code = jnp.zeros((LANES, elem_count), f32)
-    for g in range(slot_groups):
-        column = jnp.transpose(
-            jnp.concatenate([asked[g], jnp.zeros((LANES - GROUPS, LANES), f32)], 0)
-        )
-        ident = (iota((LANES, elem_count), 1) + 1).astype(f32)
-        row = iota((LANES, elem_count), 0).astype(f32)
-        for k in range(GROUPS):
-            code = jnp.where(
-                column[:, k : k + 1] == ident, row + float((g * GROUPS + k) * LANES), code
-            )
-    slot_of = sub_sum(code).astype(i32)
+    ident = (iota((LANES, elem_count), 1) + 1).astype(f32)
+    row = iota((LANES, elem_count), 0).astype(f32)
+    column = jnp.transpose(
+        jnp.concatenate(asked + [jnp.zeros((LANES - slot_rows, LANES), f32)], 0)
+    )
+    for r in range(slot_rows):
+        code = jnp.where(column[:, r : r + 1] == ident, row + float(r * LANES), code)
+    wanted_out[2:3] = sub_sum(code).astype(i32)
 
     receive(1)
     diffuse(1)
 
-    all_wait(1, val_send, val_got)
-    tables = []
-    for g in range(slot_groups):
-        total = val_got[g * per_group]
-        for m in range(1, per_group):
-            total = total + val_got[g * per_group + m]
-        tables += [wide(total[k : k + 1]) for k in range(GROUPS)]
-    tension = [gather_wide(tables, wide(ix)) for ix in lane_pieces(slot_of)]
+    all_wait(1, ans_send, ans_got)
+    answers_out[...] = ans_got[...]
+
+
+def write_out(
+    seats,
+    states,
+    answers,
+    wanted,
+    inverse,
+    forces,
+    states_out,
+    fine_out,
+    resid_out,
+    fine,
+    resid,
+    sems,
+):
+    n = answers.shape[0]
+    nx, ny, nz = fine.shape[1:]
+    bx, by, bz = nx // SBX, ny // SBY, nz // SBZ
+    plane = bx * by
+    blocks = plane * bz
+    per_group = LANES // ROWS
+    slot_groups = n // per_group
+    elem_count = forces.shape[2]
+    copies = [
+        pltpu.make_async_copy(states, states_out, sems.at[0]),
+        pltpu.make_async_copy(resid, resid_out, sems.at[1]),
+    ]
+    copies[0].start()
+
+    def fine_copy(i):
+        here = pl.ds(i * nx // PIECES, nx // PIECES)
+        return pltpu.make_async_copy(fine.at[:, here], fine_out.at[:, here], sems.at[2 + i])
+
+    tables = [wide(row) for row in row_totals(answers, LANES // seats, 3)]
+    tension = [gather_wide(tables, wide(ix)) for ix in lane_pieces(wanted[2:3])]
     force = [
-        [passive[h][i] + tension[h] * pulled[h][i] for h in range(elem_count // LANES)]
+        [
+            forces[i, :, h * LANES : (h + 1) * LANES]
+            + tension[h] * forces[3 + i, :, h * LANES : (h + 1) * LANES]
+            for h in range(elem_count // LANES)
+        ]
         for i in range(3)
     ]
-    for g in range(0, node_count, LANES):
+    for g in range(0, inverse.shape[1], LANES):
         where = inverse[:, g : g + LANES]
         index = jnp.maximum(where, 0)
         for i in range(3):
             got = jnp.where(where >= 0, gather_wide(force[i], index), 0.0)
-            resid_out[i : i + 1, g : g + LANES] = sub_sum(got)
-
-    wanted_out[0:1] = back_row
-    wanted_out[1:2] = group
-    all_wait(2, ans_send, ans_got)
-    answers_out[...] = ans_got[...]
-
-
-def write_out(states, resid, answers, wanted, states_out, fine_out, resid_out, fine, sems):
-    n, rows_each = answers.shape[:2]
-    nx, ny, nz = fine.shape[1:]
-    bx, by, bz = nx // SBX, ny // SBY, nz // SBZ
-    plane = bx * by
-    blocks = plane * bz
-    per_group = LANES // rows_each
-    slot_groups = n * rows_each // LANES
-    copies = [
-        pltpu.make_async_copy(states, states_out, sems.at[0]),
-        pltpu.make_async_copy(resid, resid_out, sems.at[1]),
-    ]
-    for c in copies:
-        c.start()
-
-    def fine_copy(i):
-        here = pl.ds(i * nx // PIECES, nx // PIECES)
-        return pltpu.make_async_copy(fine.at[:, here], fine_out.at[:, here], sems.at[2 + i])
+            resid[i : i + 1, g : g + LANES] = sub_sum(got)
+    copies[1].start()
 
     columns = [
-        jnp.transpose(
-            answers[g * per_group : (g + 1) * per_group].reshape(LANES, LANES)
-        )
+        jnp.transpose(answers[g * per_group : (g + 1) * per_group].reshape(LANES, LANES))
         for g in range(slot_groups)
     ]
     span = 32
     halves = []
     for h in range(blocks // LANES):
         cut = slice(h * LANES, (h + 1) * LANES)
-        where, which = wide(wanted[0:1, cut]), wide(wanted[1:2, cut])
+        owner, rank = wide(wanted[0:1, cut]), wide(wanted[1:2, cut])
         rows_in = []
         for c in range(3):
             value = None
-            for k in range(GROUPS):
-                first = k * span + c * SUB
-                found = gather_wide([col[first : first + SUB] for col in columns], where)
-                value = found if value is None else jnp.where(which == k, found, value)
+            for seat in range(seats):
+                pieces = [col[seat * SUB : (seat + 1) * SUB] for col in columns]
+                found = gather_wide(pieces, owner * ROWS + c)
+                value = found if value is None else jnp.where(rank == seat, found, value)
             value = 0.75 * value + 0.25 * pltpu.roll(value, 4, 0)
             swapped = jnp.where(
                 iota((SUB, LANES), 0) // 2 % 2 == 1,
@@ -897,7 +966,6 @@
     bx, by, bz = block_elem.shape
     blocks = bx * by * bz
     seats = max(2 * blocks // n, 8)
-    rows_each = seats // GROUPS
     tiles = nx // TLX
     strips = nx * ny // SUB
     ids = block_elem.transpose(0, 2, 1)
@@ -905,7 +973,7 @@
     vmem = pl.BlockSpec(memory_space=pltpu.VMEM)
     hbm = pl.BlockSpec(memory_space=pltpu.HBM)
     gates_n = NSTATE - 2
-    ways = len(DIRS)
+    halo_floats = 4 * (nx + ny + 1) * nz + 12 * nx * ny
     operands = (
         states.reshape(NSTATE, strips, SUB, nz),
         active.transpose(1, 2, 0),
@@ -934,12 +1002,13 @@
         functools.partial(body, (mx, my, mz, seats, nx, ny)),
         out_shape=(
             states_shape,
-            resid_shape,
-            jax.ShapeDtypeStruct((n, rows_each, LANES), f32),
-            jax.ShapeDtypeStruct((2, blocks), i32),
+            jax.ShapeDtypeStruct((n, ROWS, LANES), f32),
+            jax.ShapeDtypeStruct((3, blocks), i32),
+            jax.ShapeDtypeStruct((CORNERS, node_count), i32),
+            jax.ShapeDtypeStruct((6, CORNERS, elem_count), f32),
         ),
         in_specs=[hbm] * len(operands),
-        out_specs=(vmem,) * 4,
+        out_specs=(vmem,) * 5,
         scratch_shapes=[
             (pltpu.SMEM if scalar else pltpu.VMEM)(x.shape, x.dtype)
             for scalar, x in zip(in_smem, operands[1:])
@@ -949,36 +1018,36 @@
             pltpu.VMEM((stage, nx * ny, nz), f32),
             pltpu.VMEM((3, nx, ny, nz), f32),
             pltpu.VMEM((gates_n, 2, SUB, LANES), f32),
-            pltpu.VMEM((tiles, gates_n, 4, SUB, LANES), f32),
+            pltpu.VMEM((tiles, gates_n, 6, SUB, LANES), f32),
+            pltpu.VMEM((2, strips, SUB, nz), f32),
+            pltpu.VMEM((gates_n, strips, SUB, nz), f32),
             pltpu.VMEM((tiles * SUB, LANES), f32),
             pltpu.VMEM((stage, 2, 2, nx, nz), f32),
             pltpu.VMEM((stage, 2, 2, nx * ny), f32),
             pltpu.VMEM((stage, 4, 1, nz), f32),
             pltpu.VMEM((stage, 2, 1, nx * ny), f32),
-            pltpu.VMEM((stage, 2, 2 * ny, nz), f32),
-            pltpu.VMEM((stage, 2, 2, nx, nz), f32),
-            pltpu.VMEM((stage, 2, 2, nx * ny), f32),
-            pltpu.VMEM((stage, 4, 1, nz), f32),
-            pltpu.VMEM((stage, 4, 1, nx * ny), f32),
-            pltpu.VMEM((stage, 4, 1, nx * ny), f32),
-            pltpu.VMEM((6, tiles * SUB, LANES), f32),
+            pltpu.VMEM((stage, 4, 2 * ny, nz), f32),
+            pltpu.VMEM((stage, 4, 2, nx, nz), f32),
+            pltpu.VMEM((stage, 4, 2, nx * ny), f32),
+            pltpu.VMEM((stage, 8, 1, nz), f32),
+            pltpu.VMEM((stage, 8, 1, nx * ny), f32),
+            pltpu.VMEM((stage, 8, 1, nx * ny), f32),
+            pltpu.VMEM((12, tiles * SUB, LANES), f32),
+            pltpu.VMEM((halo_floats // LANES, 1, LANES), f32),
             pltpu.VMEM((nx * ny, nz), f32),
-            pltpu.VMEM((n * GROUPS, LANES), i32),
-            pltpu.VMEM((CORNERS, node_count), i32),
-            pltpu.VMEM((n, GROUPS, LANES), f32),
-            pltpu.VMEM((n, GROUPS, LANES), f32),
-            pltpu.VMEM((n, GROUPS, LANES), f32),
-            pltpu.VMEM((n, GROUPS, LANES), f32),
-            pltpu.VMEM((n, rows_each, LANES), f32),
-            pltpu.VMEM((n, rows_each, LANES), f32),
+            pltpu.VMEM((n, LANES), i32),
+            pltpu.VMEM((n, 1, LANES), f32),
+            pltpu.VMEM((n, 1, LANES), f32),
+            pltpu.VMEM((n, ROWS, LANES), f32),
+            pltpu.VMEM((n, ROWS, LANES), f32),
             pltpu.SemaphoreType.DMA((2 * tiles,)),
             pltpu.SemaphoreType.DMA((len(operands) - 1,)),
-            pltpu.SemaphoreType.DMA((stage, ways)),
-            pltpu.SemaphoreType.DMA((stage, ways)),
-            pltpu.SemaphoreType.DMA((6,)),
-            pltpu.SemaphoreType.DMA((6,)),
-            pltpu.SemaphoreType.DMA((3,)),
-            pltpu.SemaphoreType.DMA((3,)),
+            pltpu.SemaphoreType.DMA((stage,)),
+            pltpu.SemaphoreType.DMA((stage,)),
+            pltpu.SemaphoreType.DMA,
+            pltpu.SemaphoreType.DMA,
+            pltpu.SemaphoreType.DMA((2,)),
+            pltpu.SemaphoreType.DMA((2,)),
         ],
         compiler_params=pltpu.CompilerParams(
             collective_id=0, has_side_effects=True, vmem_limit_bytes=20 * 1024 * 1024
@@ -986,12 +1055,13 @@
         name="step",
     )(*(pltpu.with_memory_space_constraint(a, pltpu.HBM) for a in operands))
     results = pl.pallas_call(
-        write_out,
+        functools.partial(write_out, seats),
         out_shape=(states_shape, fine_shape, resid_shape),
-        in_specs=[vmem] * 4,
+        in_specs=[vmem] * 5,
         out_specs=(hbm,) * 3,
         scratch_shapes=[
             pltpu.VMEM((3, nx, ny, nz), f32),
+            pltpu.VMEM((3, node_count), f32),
             pltpu.SemaphoreType.DMA((2 + PIECES,)),
         ],
         compiler_params=pltpu.CompilerParams(vmem_limit_bytes=20 * 1024 * 1024),

time: 20.5 us -> 19.2 us (0.937)
  Pallas kernels: 19.8 us -> 18.4 us
    pallas_call x1, Pallas kernels: 18.1 us -> 16.6 us  [shards(): pl.pallas_call(functools.partial(body, (mx, my, mz, seats, nx, ny)), out_...]
where the time goes in v4:
time: 19.2 us; the launch traced here: 19 us
  Pallas kernels  18.4 us (96%)
  between operations  0.65 us (3%)
    pallas_call x1, Pallas kernels, shards(): pl.pallas_call(functools.partial(body, (mx, my, mz, seats, nx, ny)), out_...  16.6 us
    pallas_call x1, Pallas kernels, shards(): pl.pallas_call(functools.partial(write_out, seats), out_shape=(states_sha...  1.76 us

profile of v4, /device:TPU:0, one launch (start us, length us, event | category | flops | bytes accessed | tf_op | source)
XLA Modules:
  0.0 19.0 jit_solution(8838451976179193563)
XLA Ops:
  0.6 16.6 %step.1 = (f32[19,32,8,128]{3,2,1,0:T(8,128)S(1)}, f32[32,4,128]{2,1,0:T(4,128)S(1)}, s32[3,256]{1,0:T(4,128)S(1)}, s32[8,512]{1,0:T(8,128)S(1)}, f32[6,8,256]{2,1,0:T(8,128)S(1)}) custom-call(f32[19,32,8,128]{3,2,1,0:T(8,128)} %bitcast.7, s32[1,1,2]{2,1,0:T(1,128)} %bitcast.11, s32[1,1,2]{2,1,0:T(1,128)} %bitcast.12, f32[2,64]{1,0:T(2,128)} %refs_4_.1, ...), custom_call_target="tpu_custom_call" | custom-call | tf_op jit(solution)/shard_map/step/pallas_call | solution.py:1001
  17.3 1.8 %write.1 = (f32[19,32,8,128]{3,2,1,0:T(8,128)}, f32[3,16,16,128]{3,2,1,0:T(8,128)}, f32[3,512]{1,0:T(4,128)}) custom-call(f32[19,32,8,128]{3,2,1,0:T(8,128)S(1)} %get-tuple-element.11.states, f32[32,4,128]{2,1,0:T(4,128)S(1)} %get-tuple-element.12.answers, s32[3,256]{1,0:T(4,128)S(1)} %get-tuple-element.13.wanted, s32[8,512]{1,0:T(8,128)S(1)} %get-tuple-element.14.inverse, ...), custom_call_target="tpu_custom_call" | custom-call | tf_op jit(solution)/shard_map/write/pallas_call | solution.py:1057

commit v5 on v4

--- a/solution.py
+++ b/solution.py
@@ -18,7 +18,8 @@
 LANES = 128
 SUB = 8
 CORNERS = 8
-ROWS = 4
+GROUPS = 4
+SPAN = 32
 PIECES = 4
 f32 = jnp.float32
 bf16 = jnp.bfloat16
@@ -82,16 +83,6 @@
 
 def lane_pieces(x):
     return [x[:, h : h + LANES] for h in range(0, x.shape[1], LANES)]
-
-
-def row_totals(got, per_row, row):
-    totals = []
-    for r in range(0, got.shape[0], per_row):
-        total = got[r, row : row + 1]
-        for m in range(1, per_row):
-            total = total + got[r + m, row : row + 1]
-        totals.append(total)
-    return totals
 
 
 def sub_sum(x):
@@ -171,7 +162,8 @@
     tiles = nx // TLX
     node_count = node_disp.shape[1]
     elem_count = elem_node.shape[1]
-    per_group = LANES // ROWS
+    rows_each = seats // GROUPS
+    per_group = LANES // rows_each
     slot_groups = n // per_group
     per_row = LANES // seats
     slot_rows = n // per_row
@@ -213,6 +205,16 @@
     def load(i):
         here = pl.ds(i * chunk, chunk)
         return pltpu.make_async_copy(states.at[:, here], held.at[:, here], load_sem.at[i])
+
+    for ref in (halo_x, halo_y, halo_z, edge_xy, edge_xz, edge_yz):
+        used = ref.shape[1] // 2
+        ref[:, :used] = jnp.zeros((ref.shape[0], used) + ref.shape[2:], f32)
+    halo_coef[:6] = jnp.zeros((6,) + halo_coef.shape[1:], f32)
+
+    barrier = pltpu.get_barrier_semaphore()
+    each_other(
+        lambda to: pl.semaphore_signal(barrier, inc=1, device_id=to, device_id_type=MESH)
+    )
 
     small_loads = [
         pltpu.make_async_copy(src, dst, small_sem.at[i])
@@ -222,16 +224,6 @@
         c.start()
     for i in range(strips // chunk):
         load(i).start()
-
-    for ref in (halo_x, halo_y, halo_z, edge_xy, edge_xz, edge_yz):
-        used = ref.shape[1] // 2
-        ref[:, :used] = jnp.zeros((ref.shape[0], used) + ref.shape[2:], f32)
-    halo_coef[:6] = jnp.zeros((6,) + halo_coef.shape[1:], f32)
-
-    barrier = pltpu.get_barrier_semaphore()
-    each_other(
-        lambda to: pl.semaphore_signal(barrier, inc=1, device_id=to, device_id_type=MESH)
-    )
 
     for c in small_loads:
         c.wait()
@@ -377,27 +369,29 @@
     offset = (me % per_row) * seats
     hit = owner == iota((n, blocks), 0)
     place = onehot(iota((LANES, blocks), 0) == rank + offset)
-    sent = jnp.concatenate(
-        [
-            jnp.where(hit, (local + 1).astype(f32), 0.0),
-            jnp.where(hit, (iota((1, blocks), 1) + 1).astype(f32), 0.0),
-        ],
-        0,
+    sent = mm(jnp.where(hit, (local + 1).astype(f32), 0.0).astype(bf16), place, NT)
+    ids_send[...] = sent.reshape(n, 1, LANES)
+    group, seat_row = rank % GROUPS, rank // GROUPS
+    number = jnp.where(
+        group == iota((SUB, blocks), 0), (iota((SUB, blocks), 1) + 1).astype(f32), 0.0
     ).astype(bf16)
-    sent = mm(sent, place, NT)
-    ids_send[...] = sent[:n].reshape(n, 1, LANES)
-    block_at = sent[n:].astype(i32) - 1
-    in_plane = block_at % plane
-    slot_pos[...] = jnp.where(
-        block_at >= 0,
-        (block_at // plane // 2) * LANES
-        + (in_plane // by) * ny
-        + (in_plane % by) * SBY
-        + (block_at // plane) % 2,
-        -1,
-    )
-    wanted_out[0:1] = owner
-    wanted_out[1:2] = rank
+    seat_place = owner * rows_each + seat_row
+    for g in range(slot_groups):
+        block_at = (
+            mm(number, onehot(iota((LANES, blocks), 0) + g * LANES == seat_place), NT).astype(i32)
+            - 1
+        )
+        in_plane = block_at % plane
+        slot_pos[g] = jnp.where(
+            block_at >= 0,
+            (block_at // plane // 2) * LANES
+            + (in_plane // by) * ny
+            + (in_plane % by) * SBY
+            + (block_at // plane) % 2,
+            -1,
+        )
+    wanted_out[0:1] = seat_place
+    wanted_out[1:2] = group
 
     raw = jnp.concatenate(parts(weight_ref[...].reshape(flat_in), 2), 0).astype(bf16)
     put = onehot(iota((by, bx * ny), 1) % ny == iota((by, bx * ny), 0) * SBY)
@@ -773,22 +767,26 @@
         for b in range(0, bz, 2)
     ]
     value_rows = []
-    for r in range(0, n, SUB):
-        where = slot_pos[r : r + SUB]
+    for g in range(slot_groups):
+        where = slot_pos[g]
         value_rows.append(
             jnp.where(where >= 0, gather_wide(tables, jnp.maximum(where, 0)), 0.0)
         )
 
     all_wait(0, ids_send, ids_got)
-    asked = row_totals(ids_got, per_row, 0)
+    asked = []
+    for r in range(0, n, per_row):
+        total = ids_got[r]
+        for m in range(1, per_row):
+            total = total + ids_got[r + m]
+        asked.append(total)
     asked_wide = [wide(row) for row in asked]
     place = iota((SUB, LANES), 1)
-    which = place % ROWS
     for g in range(slot_groups):
-        device_at = g * per_group + place // ROWS
+        device_at = g * per_group + place // rows_each
         rows_out = []
-        for seat in range(seats):
-            source = (device_at % per_row) * seats + seat
+        for k in range(GROUPS):
+            source = (device_at % per_row) * seats + (place % rows_each) * GROUPS + k
             where = None
             for r in range(g * per_group // per_row, -(-(g + 1) * per_group // per_row)):
                 found = lane_gather(asked_wide[r], source)
@@ -796,22 +794,12 @@
                     found if where is None else jnp.where(device_at // per_row == r, found, where)
                 )
             where = jnp.maximum(where.astype(i32) - 1, 0)
-            low, high = where % LANES, where // LANES
-            value = None
-            for c in range(3):
-                for h in range(elem_count // LANES):
-                    found = lane_gather(disp[c][h], low)
-                    value = (
-                        found
-                        if value is None
-                        else jnp.where((which == c) & (high == h), found, value)
-                    )
-            rows_out.append(value)
-        rows_out += [jnp.zeros((SUB, LANES), f32)] * (LANES // SUB - seats)
+            rows_out += [gather_wide(disp[c], where) for c in range(3)]
+            rows_out.append(wide(value_rows[g][k : k + 1]))
         answer = jnp.transpose(jnp.concatenate(rows_out, 0))
-        ans_send[g * per_group : (g + 1) * per_group] = answer.reshape(per_group, ROWS, LANES)
-    for r in range(0, n, SUB):
-        ans_send[r : r + SUB, 3:4] = value_rows[r // SUB].reshape(SUB, 1, LANES)
+        ans_send[g * per_group : (g + 1) * per_group] = answer.reshape(
+            per_group, rows_each, LANES
+        )
     all_start(1, ans_send, ans_got)
     over_chunks(ionic_between)
     prepare(1)
@@ -820,12 +808,18 @@
 
     code = jnp.zeros((LANES, elem_count), f32)
     ident = (iota((LANES, elem_count), 1) + 1).astype(f32)
-    row = iota((LANES, elem_count), 0).astype(f32)
+    row = iota((LANES, 1), 0)
+
+    def arrival(lane, r):
+        seat = lane % seats
+        lane = (r * per_row + lane // seats) * rows_each + seat // GROUPS
+        return ((lane // LANES * GROUPS + seat % GROUPS) * LANES + lane % LANES).astype(f32)
+
     column = jnp.transpose(
         jnp.concatenate(asked + [jnp.zeros((LANES - slot_rows, LANES), f32)], 0)
     )
     for r in range(slot_rows):
-        code = jnp.where(column[:, r : r + 1] == ident, row + float(r * LANES), code)
+        code = jnp.where(column[:, r : r + 1] == ident, arrival(row, r), code)
     wanted_out[2:3] = sub_sum(code).astype(i32)
 
     receive(1)
@@ -836,7 +830,6 @@
 
 
 def write_out(
-    seats,
     states,
     answers,
     wanted,
@@ -849,12 +842,12 @@
     resid,
     sems,
 ):
-    n = answers.shape[0]
+    n, rows_each = answers.shape[:2]
     nx, ny, nz = fine.shape[1:]
     bx, by, bz = nx // SBX, ny // SBY, nz // SBZ
     plane = bx * by
     blocks = plane * bz
-    per_group = LANES // ROWS
+    per_group = LANES // rows_each
     slot_groups = n // per_group
     elem_count = forces.shape[2]
     copies = [
@@ -867,7 +860,16 @@
         here = pl.ds(i * nx // PIECES, nx // PIECES)
         return pltpu.make_async_copy(fine.at[:, here], fine_out.at[:, here], sems.at[2 + i])
 
-    tables = [wide(row) for row in row_totals(answers, LANES // seats, 3)]
+    columns = [
+        jnp.transpose(answers[g * per_group : (g + 1) * per_group].reshape(LANES, LANES))
+        for g in range(slot_groups)
+    ]
+
+    tables = [
+        wide(col[k * SPAN + 3 * CORNERS : k * SPAN + 3 * CORNERS + 1])
+        for col in columns
+        for k in range(GROUPS)
+    ]
     tension = [gather_wide(tables, wide(ix)) for ix in lane_pieces(wanted[2:3])]
     force = [
         [
@@ -885,22 +887,17 @@
             resid[i : i + 1, g : g + LANES] = sub_sum(got)
     copies[1].start()
 
-    columns = [
-        jnp.transpose(answers[g * per_group : (g + 1) * per_group].reshape(LANES, LANES))
-        for g in range(slot_groups)
-    ]
-    span = 32
     halves = []
     for h in range(blocks // LANES):
         cut = slice(h * LANES, (h + 1) * LANES)
-        owner, rank = wide(wanted[0:1, cut]), wide(wanted[1:2, cut])
+        where, which = wide(wanted[0:1, cut]), wide(wanted[1:2, cut])
         rows_in = []
         for c in range(3):
             value = None
-            for seat in range(seats):
-                pieces = [col[seat * SUB : (seat + 1) * SUB] for col in columns]
-                found = gather_wide(pieces, owner * ROWS + c)
-                value = found if value is None else jnp.where(rank == seat, found, value)
+            for k in range(GROUPS):
+                first = k * SPAN + c * CORNERS
+                found = gather_wide([col[first : first + CORNERS] for col in columns], where)
+                value = found if value is None else jnp.where(which == k, found, value)
             value = 0.75 * value + 0.25 * pltpu.roll(value, 4, 0)
             swapped = jnp.where(
                 iota((SUB, LANES), 0) // 2 % 2 == 1,
@@ -919,7 +916,7 @@
         )
     around = jnp.transpose(jnp.concatenate(stacked, 0))
     lane = iota((SUB, nz), 1)
-    strip_lane = lane // SBZ * span
+    strip_lane = lane // SBZ * SPAN
     xi = ((lane % SBZ).astype(f32) + 0.5) / SBZ
     for p in range(bx):
         near = around[p * by : (p + 1) * by]
@@ -968,6 +965,7 @@
     seats = max(2 * blocks // n, 8)
     tiles = nx // TLX
     strips = nx * ny // SUB
+    rows_each = seats // GROUPS
     ids = block_elem.transpose(0, 2, 1)
     weight = block_weight.transpose(0, 2, 1)
     vmem = pl.BlockSpec(memory_space=pltpu.VMEM)
@@ -1002,7 +1000,7 @@
         functools.partial(body, (mx, my, mz, seats, nx, ny)),
         out_shape=(
             states_shape,
-            jax.ShapeDtypeStruct((n, ROWS, LANES), f32),
+            jax.ShapeDtypeStruct((n, rows_each, LANES), f32),
             jax.ShapeDtypeStruct((3, blocks), i32),
             jax.ShapeDtypeStruct((CORNERS, node_count), i32),
             jax.ShapeDtypeStruct((6, CORNERS, elem_count), f32),
@@ -1035,11 +1033,11 @@
             pltpu.VMEM((12, tiles * SUB, LANES), f32),
             pltpu.VMEM((halo_floats // LANES, 1, LANES), f32),
             pltpu.VMEM((nx * ny, nz), f32),
-            pltpu.VMEM((n, LANES), i32),
+            pltpu.VMEM((n * rows_each // LANES, SUB, LANES), i32),
             pltpu.VMEM((n, 1, LANES), f32),
             pltpu.VMEM((n, 1, LANES), f32),
-            pltpu.VMEM((n, ROWS, LANES), f32),
-            pltpu.VMEM((n, ROWS, LANES), f32),
+            pltpu.VMEM((n, rows_each, LANES), f32),
+            pltpu.VMEM((n, rows_each, LANES), f32),
             pltpu.SemaphoreType.DMA((2 * tiles,)),
             pltpu.SemaphoreType.DMA((len(operands) - 1,)),
             pltpu.SemaphoreType.DMA((stage,)),
@@ -1055,7 +1053,7 @@
         name="step",
     )(*(pltpu.with_memory_space_constraint(a, pltpu.HBM) for a in operands))
     results = pl.pallas_call(
-        functools.partial(write_out, seats),
+        write_out,
         out_shape=(states_shape, fine_shape, resid_shape),
         in_specs=[vmem] * 5,
         out_specs=(hbm,) * 3,

time: 19.2 us -> 18.9 us (0.984)
  Pallas kernels: 18.4 us -> 18.1 us
    pallas_call x1, Pallas kernels: 16.6 us -> 16.4 us  [shards(): pl.pallas_call(functools.partial(body, (mx, my, mz, seats, nx, ny)), out_...]
where the time goes in v5:
time: 18.9 us; the launch traced here: 18.8 us
  Pallas kernels  18.1 us (96%)
  between operations  0.65 us (3%)
    pallas_call x1, Pallas kernels, shards(): pl.pallas_call(functools.partial(body, (mx, my, mz, seats, nx, ny)), out_...  16.4 us
    pallas_call x1, Pallas kernels, shards(): pl.pallas_call(write_out, out_shape=(states_shape, fine_shape, resid_shap...  1.74 us

profile of v5, /device:TPU:0, one launch (start us, length us, event | category | flops | bytes accessed | tf_op | source)
XLA Modules:
  0.0 18.8 jit_solution(12947974293824304654)
XLA Ops:
  0.6 16.4 %step.1 = (f32[19,32,8,128]{3,2,1,0:T(8,128)S(1)}, f32[32,4,128]{2,1,0:T(4,128)S(1)}, s32[3,256]{1,0:T(4,128)S(1)}, s32[8,512]{1,0:T(8,128)S(1)}, f32[6,8,256]{2,1,0:T(8,128)S(1)}) custom-call(f32[19,32,8,128]{3,2,1,0:T(8,128)} %bitcast.7, s32[1,1,2]{2,1,0:T(1,128)} %bitcast.11, s32[1,1,2]{2,1,0:T(1,128)} %bitcast.12, f32[2,64]{1,0:T(2,128)} %refs_4_.1, ...), custom_call_target="tpu_custom_call" | custom-call | tf_op jit(solution)/shard_map/step/pallas_call | solution.py:999
  17.0 1.7 %write.1 = (f32[19,32,8,128]{3,2,1,0:T(8,128)}, f32[3,16,16,128]{3,2,1,0:T(8,128)}, f32[3,512]{1,0:T(4,128)}) custom-call(f32[19,32,8,128]{3,2,1,0:T(8,128)S(1)} %get-tuple-element.11.states, f32[32,4,128]{2,1,0:T(4,128)S(1)} %get-tuple-element.12.answers, s32[3,256]{1,0:T(4,128)S(1)} %get-tuple-element.13.wanted, s32[8,512]{1,0:T(8,128)S(1)} %get-tuple-element.14.inverse, ...), custom_call_target="tpu_custom_call" | custom-call | tf_op jit(solution)/shard_map/write/pallas_call | solution.py:1055

commit v6 on v5

--- a/solution.py
+++ b/solution.py
@@ -120,6 +120,7 @@
         held,
         vs,
         flux,
+        grad,
         gate_const,
         tile_const,
         sums,
@@ -539,6 +540,18 @@
     def coef_row(ref, t, k):
         return ref[t * SUB + k : t * SUB + k + 1, :]
 
+    def slopes(stage):
+        v = vs[stage].reshape(nx, ny, nz)
+        zero = jnp.zeros((1, ny, nz), f32)
+        row, lane = iota((1, ny, nz), 1), iota((1, 1, nz), 2)
+        grad[0] = jnp.concatenate([v[1:], zero], 0) - jnp.concatenate([zero, v[:-1]], 0)
+        grad[1] = jnp.where(row == ny - 1, 0.0, pltpu.roll(v, ny - 1, 1)) - jnp.where(
+            row == 0, 0.0, pltpu.roll(v, 1, 1)
+        )
+        grad[2] = jnp.where(lane == nz - 1, 0.0, pltpu.roll(v, nz - 1, 2)) - jnp.where(
+            lane == 0, 0.0, pltpu.roll(v, 1, 2)
+        )
+
     def diffuse(stage):
         v = vs[stage].reshape(nx, ny, nz)
         lane = iota((1, nz), 1)
@@ -650,7 +663,16 @@
             return up - down
 
         edges = turned[...].reshape(nx, ny, nz)
-        gx, gy, gz = diff_x(v, *px), diff_y(v, *py), diff_z(v, edges)
+        row, lane3 = iota((1, ny, nz), 1), iota((1, 1, nz), 2)
+        first_x, last_x = grad[0, 0] - px[0], grad[0, nx - 1] + px[1]
+        gx = jnp.concatenate([first_x[None], grad[0, 1 : nx - 1], last_x[None]], 0)
+        gy = grad[1] + jnp.where(
+            row == ny - 1,
+            py[1].reshape(nx, 1, nz),
+            jnp.where(row == 0, -py[0].reshape(nx, 1, nz), 0.0),
+        )
+        side = jnp.where(lane3 == nz - 1, 1.0, jnp.where(lane3 == 0, -1.0, 0.0))
+        gz = grad[2] + edges * side
         for t in range(tiles):
             span = slice(t * TLX, (t + 1) * TLX)
             xx, yy, zz, xy, xz_, yz_ = (
@@ -679,6 +701,7 @@
     send_coef()
 
 
+    slopes(0)
     over_chunks(ionic_before)
     nodes = elem_node[...]
     disp = []
@@ -804,6 +827,7 @@
     over_chunks(ionic_between)
     prepare(1)
     send(1)
+    slopes(1)
     over_chunks(ionic_after)
 
     code = jnp.zeros((LANES, elem_count), f32)
@@ -1015,6 +1039,7 @@
             pltpu.VMEM((NSTATE, strips, SUB, nz), f32),
             pltpu.VMEM((stage, nx * ny, nz), f32),
             pltpu.VMEM((3, nx, ny, nz), f32),
+            pltpu.VMEM((3, nx, ny, nz), f32),
             pltpu.VMEM((gates_n, 2, SUB, LANES), f32),
             pltpu.VMEM((tiles, gates_n, 6, SUB, LANES), f32),
             pltpu.VMEM((2, strips, SUB, nz), f32),

time: 18.9 us -> 18.9 us (level)
  no operation moved by 1% of the time
where the time goes in v6:
time: 18.9 us; the launch traced here: 18.8 us
  Pallas kernels  18.1 us (96%)
  between operations  0.65 us (3%)
    pallas_call x1, Pallas kernels, shards(): pl.pallas_call(functools.partial(body, (mx, my, mz, seats, nx, ny)), out_...  16.4 us
    pallas_call x1, Pallas kernels, shards(): pl.pallas_call(write_out, out_shape=(states_shape, fine_shape, resid_shap...  1.74 us

profile of v6, /device:TPU:0, one launch (start us, length us, event | category | flops | bytes accessed | tf_op | source)
XLA Modules:
  0.0 18.8 jit_solution(11012359481001378589)
XLA Ops:
  0.6 16.4 %step.1 = (f32[19,32,8,128]{3,2,1,0:T(8,128)S(1)}, f32[32,4,128]{2,1,0:T(4,128)S(1)}, s32[3,256]{1,0:T(4,128)S(1)}, s32[8,512]{1,0:T(8,128)S(1)}, f32[6,8,256]{2,1,0:T(8,128)S(1)}) custom-call(f32[19,32,8,128]{3,2,1,0:T(8,128)} %bitcast.7, s32[1,1,2]{2,1,0:T(1,128)} %bitcast.11, s32[1,1,2]{2,1,0:T(1,128)} %bitcast.12, f32[2,64]{1,0:T(2,128)} %refs_4_.1, ...), custom_call_target="tpu_custom_call" | custom-call | tf_op jit(solution)/shard_map/step/pallas_call | solution.py:1023
  17.0 1.7 %write.1 = (f32[19,32,8,128]{3,2,1,0:T(8,128)}, f32[3,16,16,128]{3,2,1,0:T(8,128)}, f32[3,512]{1,0:T(4,128)}) custom-call(f32[19,32,8,128]{3,2,1,0:T(8,128)S(1)} %get-tuple-element.11.states, f32[32,4,128]{2,1,0:T(4,128)S(1)} %get-tuple-element.12.answers, s32[3,256]{1,0:T(4,128)S(1)} %get-tuple-element.13.wanted, s32[8,512]{1,0:T(8,128)S(1)} %get-tuple-element.14.inverse, ...), custom_call_target="tpu_custom_call" | custom-call | tf_op jit(solution)/shard_map/write/pallas_call | solution.py:1080

commit v7 on v5

--- a/solution.py
+++ b/solution.py
@@ -187,11 +187,11 @@
 
     wrapped = [[jnp.where(p + s >= m, p + s - m, p + s) for s in range(m)] for p, m in zip(at, counts)]
 
-    def each_other(go):
+    def each_other(go, keep=lambda k: True):
         if n <= 64:
-            for step in others():
+            for step in (x for k, x in enumerate(others()) if keep(k)):
                 go(tuple(wrapped[d][s] for d, s in enumerate(step)))
-        else:
+        elif keep(0):
 
             def one(k, carry):
                 flat = (me + k) % n
@@ -510,8 +510,9 @@
             device_id_type=MESH,
         ).wait()
 
-    def all_start(kind, src, dst):
-        dst[pl.ds(me, 1)] = src[pl.ds(me, 1)]
+    def all_start(kind, src, dst, keep=lambda k: True):
+        if keep(0):
+            dst[pl.ds(me, 1)] = src[pl.ds(me, 1)]
 
         def go(to):
             flat = (to[0] * my + to[1]) * mz + to[2]
@@ -524,7 +525,7 @@
                 device_id_type=MESH,
             ).start()
 
-        each_other(go)
+        each_other(go, keep)
 
     def all_wait(kind, src, dst):
         pltpu.make_async_remote_copy(
@@ -674,8 +675,10 @@
 
     prepare(0)
     pl.semaphore_wait(barrier, n - 1)
-    all_start(0, ids_send, ids_got)
+    half = n // 2
+    all_start(0, ids_send, ids_got, lambda k: k < half)
     send(0)
+    all_start(0, ids_send, ids_got, lambda k: k >= half)
     send_coef()
 
 

time: 18.9 us -> 18.9 us (level)
  no operation moved by 1% of the time
where the time goes in v7:
time: 18.9 us; the launch traced here: 18.8 us
  Pallas kernels  18.1 us (96%)
  between operations  0.65 us (3%)
    pallas_call x1, Pallas kernels, shards(): pl.pallas_call(functools.partial(body, (mx, my, mz, seats, nx, ny)), out_...  16.4 us
    pallas_call x1, Pallas kernels, shards(): pl.pallas_call(write_out, out_shape=(states_shape, fine_shape, resid_shap...  1.74 us

profile of v7, /device:TPU:0, one launch (start us, length us, event | category | flops | bytes accessed | tf_op | source)
XLA Modules:
  0.0 18.8 jit_solution(5371848705380007672)
XLA Ops:
  0.6 16.4 %step.1 = (f32[19,32,8,128]{3,2,1,0:T(8,128)S(1)}, f32[32,4,128]{2,1,0:T(4,128)S(1)}, s32[3,256]{1,0:T(4,128)S(1)}, s32[8,512]{1,0:T(8,128)S(1)}, f32[6,8,256]{2,1,0:T(8,128)S(1)}) custom-call(f32[19,32,8,128]{3,2,1,0:T(8,128)} %bitcast.7, s32[1,1,2]{2,1,0:T(1,128)} %bitcast.11, s32[1,1,2]{2,1,0:T(1,128)} %bitcast.12, f32[2,64]{1,0:T(2,128)} %refs_4_.1, ...), custom_call_target="tpu_custom_call" | custom-call | tf_op jit(solution)/shard_map/step/pallas_call | solution.py:1002
  17.0 1.7 %write.1 = (f32[19,32,8,128]{3,2,1,0:T(8,128)}, f32[3,16,16,128]{3,2,1,0:T(8,128)}, f32[3,512]{1,0:T(4,128)}) custom-call(f32[19,32,8,128]{3,2,1,0:T(8,128)S(1)} %get-tuple-element.11.states, f32[32,4,128]{2,1,0:T(4,128)S(1)} %get-tuple-element.12.answers, s32[3,256]{1,0:T(4,128)S(1)} %get-tuple-element.13.wanted, s32[8,512]{1,0:T(8,128)S(1)} %get-tuple-element.14.inverse, ...), custom_call_target="tpu_custom_call" | custom-call | tf_op jit(solution)/shard_map/write/pallas_call | solution.py:1058
